TPU v7x, 32 devices: a whole 2x2x4 slice. The times are simulated.
32 devices in a mesh: dp: 8 (over z, y), tm: 4 (over x, core).
Axes of the slice: x: 2, y: 2, z: 4, core: 2. Of those that a mesh axis runs over, the one named last changes fastest.
Arguments:
- inputs: bfloat16 [8, 4096, 512], P('dp', 'tm'), may hold values from -6 to 6
- w_query: bfloat16 [512, 512], replicated, may hold values from -0.25 to 0.25
- w_key: bfloat16 [512, 512], replicated, may hold values from -0.25 to 0.25
- w_value: bfloat16 [512, 512], replicated, may hold values from -0.25 to 0.25
- w_out: bfloat16 [512, 512], replicated, may hold values from -0.25 to 0.25
- saved_heads: bfloat16 [8, 4096, 512], P('dp', 'tm'), may hold values from -6 to 6
- log_totals: float32 [8, 8, 4096], P('dp', None, 'tm'), may hold values from 0 to 8
- out_grad: bfloat16 [8, 4096, 512], P('dp', 'tm'), may hold values from -6 to 6
Outputs:
- input_grad: bfloat16 [8, 4096, 512], P('dp', 'tm')
- weight_grads: float32 [2048, 512], P(('dp', 'tm'))
All inputs are finite; a program needn't handle non-finite values.
Results may differ from a plain program's by a relative error of at most 0.012.
Values may be sent and summed in bfloat16 or wider, within the bound.
No kernel may reach another device: no remote copies, remote signals or barrier semaphores. Data moves between devices by JAX's collectives and lax.ppermute only.
A program may use at most 128 MiB of HBM per device.

v0:
```python
import jax
import jax.numpy as jnp
from jax import lax
from jax.sharding import PartitionSpec as P

HEADS = 8
HEAD_DIM = 64
WINDOW = 1024
SHARD_BINS = 1024
QUERY_BLOCK = 512


def passed_along(value, axis, steps):
    count = lax.axis_size(axis)
    initial, last = (max(0, -steps), min(count, count - steps))
    return lax.ppermute(value, axis, [(source, source + steps) for source in range(initial, last)])


def split_heads(matrix):
    return matrix.reshape(matrix.shape[0], HEADS, HEAD_DIM).transpose(1, 0, 2)


def join_heads(tensor):
    return tensor.transpose(1, 0, 2).reshape(tensor.shape[1], HEADS * HEAD_DIM)


def block_grads(query_heads, key_heads, value_heads, grad_heads, saved_split, total_rows, allowed):
    score_scale = HEAD_DIM ** (-0.5)

    def per_head(head_items):
        query_rows, key_rows, value_rows, grad_rows, saved_rows, lse_rows = head_items
        scores = jnp.dot(query_rows, key_rows.T, preferred_element_type=jnp.float32) * score_scale
        soft_weights = jnp.where(allowed, jnp.exp(scores - lse_rows[:, None]), 0.0)
        weights_low = soft_weights.astype(jnp.bfloat16)
        offsets = jnp.sum(grad_rows.astype(jnp.float32) * saved_rows.astype(jnp.float32), axis=1)
        prob_grad = jnp.dot(grad_rows, value_rows.T, preferred_element_type=jnp.float32)
        score_grad = (soft_weights * (prob_grad - offsets[:, None]) * score_scale).astype(
            jnp.bfloat16
        )
        grad_query = jnp.dot(score_grad, key_rows, preferred_element_type=jnp.float32)
        grad_key = jnp.dot(score_grad.T, query_rows, preferred_element_type=jnp.float32)
        grad_value = jnp.dot(weights_low.T, grad_rows, preferred_element_type=jnp.float32)
        return (grad_query, grad_key, grad_value)

    return lax.map(
        per_head, (query_heads, key_heads, value_heads, grad_heads, saved_split, total_rows)
    )


def project(matrix, weight):
    return jnp.einsum("rtd,de->rte", matrix, weight, preferred_element_type=jnp.float32).astype(
        jnp.bfloat16
    )


def back_project(matrix, weight):
    return jnp.einsum("rtd,ed->rte", matrix, weight, preferred_element_type=jnp.float32)


def outer_sum(rows, grads):
    return jnp.einsum("rte,rtd->ed", rows, grads, preferred_element_type=jnp.float32)


def on_device(inputs, w_query, w_key, w_value, w_out, saved_heads, log_totals, out_grad):
    query_full = project(inputs, w_query)
    key_full = project(inputs, w_key)
    value_full = project(inputs, w_value)
    key_prev, value_prev = passed_along((key_full, value_full), "tm", 1)
    head_grad = jnp.einsum(
        "rte,de->rtd", out_grad, w_out, preferred_element_type=jnp.float32
    ).astype(jnp.bfloat16)
    grad_out_weight = jnp.einsum(
        "rtd,rte->de", saved_heads, out_grad, preferred_element_type=jnp.float32
    )
    shard_start = lax.axis_index("tm") * SHARD_BINS
    row_ids = jnp.arange(QUERY_BLOCK, dtype=jnp.int32)[:, None]
    col_ids = jnp.arange(QUERY_BLOCK + WINDOW, dtype=jnp.int32)[None, :]

    def per_recording(rec_items):
        queries, keys_own, values_own, keys_back, values_back, grads_here, saved, totals = rec_items
        query_heads = split_heads(queries)
        key_ext = jnp.concatenate([split_heads(keys_back), split_heads(keys_own)], axis=1)
        value_ext = jnp.concatenate([split_heads(values_back), split_heads(values_own)], axis=1)
        grad_split = split_heads(grads_here)
        saved_split = split_heads(saved)
        key_acc = jnp.zeros((HEADS, WINDOW + SHARD_BINS, HEAD_DIM), jnp.float32)
        value_acc = jnp.zeros((HEADS, WINDOW + SHARD_BINS, HEAD_DIM), jnp.float32)
        query_parts = []
        for block in range(SHARD_BINS // QUERY_BLOCK):
            start = block * QUERY_BLOCK
            stop = start + QUERY_BLOCK + WINDOW
            query_pos = shard_start + start + row_ids
            key_pos = shard_start + start - WINDOW + col_ids
            allowed = (key_pos <= query_pos) & (key_pos > query_pos - WINDOW) & (key_pos >= 0)
            grad_query, grad_key, grad_value = block_grads(
                query_heads[:, start : start + QUERY_BLOCK],
                key_ext[:, start:stop],
                value_ext[:, start:stop],
                grad_split[:, start : start + QUERY_BLOCK],
                saved_split[:, start : start + QUERY_BLOCK],
                totals[:, start : start + QUERY_BLOCK],
                allowed,
            )
            key_acc = key_acc.at[:, start:stop].add(grad_key)
            value_acc = value_acc.at[:, start:stop].add(grad_value)
            query_parts.append(grad_query)
        query_grad = join_heads(jnp.concatenate(query_parts, axis=1))
        return (
            query_grad,
            join_heads(key_acc[:, :WINDOW]),
            join_heads(key_acc[:, WINDOW:]),
            join_heads(value_acc[:, :WINDOW]),
            join_heads(value_acc[:, WINDOW:]),
        )

    query_grad, key_send, key_mine, value_send, value_mine = lax.map(
        per_recording,
        (
            query_full,
            key_full,
            value_full,
            key_prev,
            value_prev,
            head_grad,
            saved_heads,
            log_totals,
        ),
    )
    grad_query_full = query_grad.astype(jnp.bfloat16)
    key_near = key_mine.astype(jnp.bfloat16)
    value_near = value_mine.astype(jnp.bfloat16)
    key_far_send = key_send.astype(jnp.bfloat16)
    value_far_send = value_send.astype(jnp.bfloat16)
    near_sum = (
        back_project(grad_query_full, w_query)
        + back_project(key_near, w_key)
        + back_project(value_near, w_value)
    )
    key_far, value_far = passed_along((key_far_send, value_far_send), "tm", -1)
    input_grad = (
        near_sum + back_project(key_far, w_key) + back_project(value_far, w_value)
    ).astype(jnp.bfloat16)
    key_weight = outer_sum(inputs, key_near) + outer_sum(inputs, key_far)
    value_weight = outer_sum(inputs, value_near) + outer_sum(inputs, value_far)
    local_grads = jnp.concatenate(
        [outer_sum(inputs, grad_query_full), key_weight, value_weight, grad_out_weight], axis=0
    )
    weight_grads = lax.psum_scatter(local_grads, ("dp", "tm"), scatter_dimension=0, tiled=True)
    return (input_grad, weight_grads)


def solution(mesh):
    in_specs = (
        P("dp", "tm", None),
        P(),
        P(),
        P(),
        P(),
        P("dp", "tm", None),
        P("dp", None, "tm"),
        P("dp", "tm", None),
    )
    out_specs = (P("dp", "tm", None), P(("dp", "tm"), None))
    return jax.shard_map(
        on_device, mesh=mesh, in_specs=in_specs, out_specs=out_specs, check_vma=False
    )
```

profile of v0, /device:TPU:0, one launch (start us, length us, event | category | flops | bytes accessed | tf_op | source)
XLA Modules:
  0.0 462.2 jit_solution(17614081635905197604)
XLA Ops:
  11.2 3.4 collective-permute-start.1
  17.3 4.5 collective-permute-start
  21.9 2.8 copy.21
  36.5 3.4 fusion.69
  47.0 8.8 %pad_maximum_fusion.1 = (bf16[8,1536,64]{2,1,0:T(8,128)(2,1)}, bf16[8,1536,64]{2,1,0:T(8,128)(2,1)}, bf16[8,1536,64]{2,1,0:T(8,128)(2,1)}, bf16[8,1536,64]{2,1,0:T(8,128)(2,1)}) fusion(bf16[8,1024,64]{2,1,0:T(8,128)(2,1)} %bitcast.227, bf16[8,1024,64]{2,1,0:T(8,128)(2,1)} %bitcast.229, bf16[8,1024,64]{2,1,0:T(8,128)(2,1)} %bitcast.228, ...), kind=kLoop, calls=%fused_computation.85 | loop fusion | flops 12582912 | bytes 10485760 | tf_op jit(solution)/shard_map/while/body/eval_jaxpr/concatenate | solution.py:83
  60.8 107.8 %while.52 = (s32[]{:T(128)}, bf16[8,512,64]{1,2,0:T(8,128)(2,1)}, f32[8,1536,64]{1,2,0:T(8,128)}, f32[8,1536,64]{1,2,0:T(8,128)}, bf16[8,512,64]{2,1,0:T(8,128)(...) while((s32[]{:T(128)}, bf16[8,512,64]{1,2,0:T(8,128)(2,1)}, ...), condition=%wide.region_2.3_spmd.clone, body=%wide.region_0.2_spmd.clone.sunk | while | flops 512884224 | bytes 29780660 | solution.py:45
  60.8 4.1 fusion.159
  74.3 4.1 fusion.159
  87.7 4.1 fusion.159
  101.2 4.1 fusion.159
  114.7 4.1 fusion.159
  128.2 4.1 fusion.159
  141.6 4.1 fusion.159
  155.1 4.1 fusion.159
  172.7 103.3 %while.53 = (s32[]{:T(128)}, bf16[8,512,64]{1,2,0:T(8,128)(2,1)S(1)}, f32[8,1536,64]{1,2,0:T(8,128)}, f32[8,1536,64]{1,2,0:T(8,128)}, bf16[8,512,64]{2,1,0:T(8,1...) while((s32[]{:T(128)}, ...), condition=%wide.region_5.6_spmd.clone, body=%wide.region_3.5_spmd.clone.sunk | while | flops 512884224 | bytes 29780660 | solution.py:45
  172.9 4.1 fusion.175
  185.8 4.1 fusion.175
  198.7 4.1 fusion.175
  211.6 4.1 fusion.175
  224.4 4.1 fusion.175
  237.4 4.1 fusion.175
  250.2 4.1 fusion.175
  263.1 4.1 fusion.175
  302.0 153.4 %reduce-scatter.2.cloned.1.call-done = f32[64,512]{1,0:T(8,128)} async-done(((f32[2048,512]{1,0:T(8,128)}), f32[64,512]{1,0:T(8,128)}) %reduce-scatter.2.cloned.1.call-update) | async-done | bytes 131088 | tf_op jit(solution)/shard_map/reduce_scatter | solution.py:148
  (255 shorter events, 205.6 us)
Async XLA Ops:
  7.2 448.2 %reduce-scatter.2.cloned.1.call-start = ((), (), s32[]{:S(2)}) async-start(), calls=%async_computation.1 | async-start | bytes 4325376 | tf_op jit(solution)/shard_map/reduce_scatter | solution.py:148
  11.2 30.4 %collective-permute-start.1 = (bf16[1,1024,512]{1,2,0:T(8,128)(2,1)}, bf16[1,1024,512]{1,2,0:T(8,128)(2,1)}, u32[]{:S(2)}, u32[]{:S(2)}) collective-permute-start(bf16[1,1024,512]{1,2,0:T(8,128)(2,1)} %bitcast.12), channel_id=1, source_target_pairs={{0,1},{1,2},{2,3},{4,5},{5,6},{6,7},{8,9},{9,10},{10,11},{12,13},{... | collective-permute-start | bytes 3145736 | tf_op jit(solution)/shard_map/ppermute | solution.py:16
  17.3 26.9 %collective-permute-start = (bf16[1,1024,512]{1,2,0:T(8,128)(2,1)}, bf16[1,1024,512]{1,2,0:T(8,128)(2,1)}, u32[]{:S(2)}, u32[]{:S(2)}) collective-permute-start(bf16[1,1024,512]{1,2,0:T(8,128)(2,1)} %bitcast.3), channel_id=1, source_target_pairs={{0,1},{1,2},{2,3},{4,5},{5,6},{6,7},{8,9},{9,10},{10,11},{12,13},{... | collective-permute-start | bytes 3145736 | tf_op jit(solution)/shard_map/ppermute | solution.py:16
  21.9 5.6 %copy-start.22 = (bf16[1,1024,512]{2,1,0:T(8,128)(2,1)S(1)}, bf16[1,1024,512]{2,1,0:T(8,128)(2,1)}, u32[]{:S(2)}) copy-start(bf16[1,1024,512]{2,1,0:T(8,128)(2,1)} %param.27) | copy-start | bytes 3145732
  35.2 4.6 copy-start.6
  66.0 4.9 %copy-start.1 = (f32[512,1536]{1,0:T(8,128)S(1)}, f32[512,1536]{1,0:T(8,128)}, u32[]{:S(2)}) copy-start(f32[512,1536]{1,0:T(8,128)} %fusion.159) | copy-start | bytes 9437188 | tf_op jit(solution)/shard_map/while/body/eval_jaxpr/while
  79.5 4.9 %copy-start.1 = (f32[512,1536]{1,0:T(8,128)S(1)}, f32[512,1536]{1,0:T(8,128)}, u32[]{:S(2)}) copy-start(f32[512,1536]{1,0:T(8,128)} %fusion.159) | copy-start | bytes 9437188 | tf_op jit(solution)/shard_map/while/body/eval_jaxpr/while
  92.9 4.9 %copy-start.1 = (f32[512,1536]{1,0:T(8,128)S(1)}, f32[512,1536]{1,0:T(8,128)}, u32[]{:S(2)}) copy-start(f32[512,1536]{1,0:T(8,128)} %fusion.159) | copy-start | bytes 9437188 | tf_op jit(solution)/shard_map/while/body/eval_jaxpr/while
  106.4 4.9 %copy-start.1 = (f32[512,1536]{1,0:T(8,128)S(1)}, f32[512,1536]{1,0:T(8,128)}, u32[]{:S(2)}) copy-start(f32[512,1536]{1,0:T(8,128)} %fusion.159) | copy-start | bytes 9437188 | tf_op jit(solution)/shard_map/while/body/eval_jaxpr/while
  119.9 4.9 %copy-start.1 = (f32[512,1536]{1,0:T(8,128)S(1)}, f32[512,1536]{1,0:T(8,128)}, u32[]{:S(2)}) copy-start(f32[512,1536]{1,0:T(8,128)} %fusion.159) | copy-start | bytes 9437188 | tf_op jit(solution)/shard_map/while/body/eval_jaxpr/while
  133.3 4.9 %copy-start.1 = (f32[512,1536]{1,0:T(8,128)S(1)}, f32[512,1536]{1,0:T(8,128)}, u32[]{:S(2)}) copy-start(f32[512,1536]{1,0:T(8,128)} %fusion.159) | copy-start | bytes 9437188 | tf_op jit(solution)/shard_map/while/body/eval_jaxpr/while
  146.8 4.9 %copy-start.1 = (f32[512,1536]{1,0:T(8,128)S(1)}, f32[512,1536]{1,0:T(8,128)}, u32[]{:S(2)}) copy-start(f32[512,1536]{1,0:T(8,128)} %fusion.159) | copy-start | bytes 9437188 | tf_op jit(solution)/shard_map/while/body/eval_jaxpr/while
  160.3 4.9 %copy-start.1 = (f32[512,1536]{1,0:T(8,128)S(1)}, f32[512,1536]{1,0:T(8,128)}, u32[]{:S(2)}) copy-start(f32[512,1536]{1,0:T(8,128)} %fusion.159) | copy-start | bytes 9437188 | tf_op jit(solution)/shard_map/while/body/eval_jaxpr/while
  178.1 4.9 %copy-start.2 = (f32[512,1536]{1,0:T(8,128)S(1)}, f32[512,1536]{1,0:T(8,128)}, u32[]{:S(2)}) copy-start(f32[512,1536]{1,0:T(8,128)} %fusion.175) | copy-start | bytes 9437188 | tf_op jit(solution)/shard_map/while/body/eval_jaxpr/while
  191.0 4.9 %copy-start.2 = (f32[512,1536]{1,0:T(8,128)S(1)}, f32[512,1536]{1,0:T(8,128)}, u32[]{:S(2)}) copy-start(f32[512,1536]{1,0:T(8,128)} %fusion.175) | copy-start | bytes 9437188 | tf_op jit(solution)/shard_map/while/body/eval_jaxpr/while
  203.9 4.8 %copy-start.2 = (f32[512,1536]{1,0:T(8,128)S(1)}, f32[512,1536]{1,0:T(8,128)}, u32[]{:S(2)}) copy-start(f32[512,1536]{1,0:T(8,128)} %fusion.175) | copy-start | bytes 9437188 | tf_op jit(solution)/shard_map/while/body/eval_jaxpr/while
  216.8 4.9 %copy-start.2 = (f32[512,1536]{1,0:T(8,128)S(1)}, f32[512,1536]{1,0:T(8,128)}, u32[]{:S(2)}) copy-start(f32[512,1536]{1,0:T(8,128)} %fusion.175) | copy-start | bytes 9437188 | tf_op jit(solution)/shard_map/while/body/eval_jaxpr/while
  229.6 4.9 %copy-start.2 = (f32[512,1536]{1,0:T(8,128)S(1)}, f32[512,1536]{1,0:T(8,128)}, u32[]{:S(2)}) copy-start(f32[512,1536]{1,0:T(8,128)} %fusion.175) | copy-start | bytes 9437188 | tf_op jit(solution)/shard_map/while/body/eval_jaxpr/while
  242.5 4.9 %copy-start.2 = (f32[512,1536]{1,0:T(8,128)S(1)}, f32[512,1536]{1,0:T(8,128)}, u32[]{:S(2)}) copy-start(f32[512,1536]{1,0:T(8,128)} %fusion.175) | copy-start | bytes 9437188 | tf_op jit(solution)/shard_map/while/body/eval_jaxpr/while
  255.4 4.9 %copy-start.2 = (f32[512,1536]{1,0:T(8,128)S(1)}, f32[512,1536]{1,0:T(8,128)}, u32[]{:S(2)}) copy-start(f32[512,1536]{1,0:T(8,128)} %fusion.175) | copy-start | bytes 9437188 | tf_op jit(solution)/shard_map/while/body/eval_jaxpr/while
  268.3 4.9 %copy-start.2 = (f32[512,1536]{1,0:T(8,128)S(1)}, f32[512,1536]{1,0:T(8,128)}, u32[]{:S(2)}) copy-start(f32[512,1536]{1,0:T(8,128)} %fusion.175) | copy-start | bytes 9437188 | tf_op jit(solution)/shard_map/while/body/eval_jaxpr/while
  276.0 5.4 %copy-start.15 = (bf16[8,512,64]{1,2,0:T(8,128)(2,1)}, bf16[8,512,64]{1,2,0:T(8,128)(2,1)S(1)}, u32[]{:S(2)}) copy-start(bf16[8,512,64]{1,2,0:T(8,128)(2,1)S(1)} %get-tuple-element.240) | copy-start | bytes 1572868
  281.5 9.2 %collective-permute-start.2 = (bf16[1,1024,512]{1,2,0:T(8,128)(2,1)S(1)}, bf16[1,1024,512]{1,2,0:T(8,128)(2,1)S(1)}, u32[]{:S(2)}, u32[]{:S(2)}) collective-permute-start(bf16[1,1024,512]{1,2,0:T(8,128)(2,1)S(1)} %bitcast.242), channel_id=1, source_target_pairs={{1,0},{2,1},{3,2},{5,4},{6,5},{7,6},{9,8},{10,9},{11,10},{13,12},{... | collective-permute-start | bytes 3145736 | tf_op jit(solution)/shard_map/ppermute | solution.py:16
  285.7 5.9 %collective-permute-start.3 = (bf16[1,1024,512]{1,2,0:T(8,128)(2,1)S(1)}, bf16[1,1024,512]{1,2,0:T(8,128)(2,1)S(1)}, u32[]{:S(2)}, u32[]{:S(2)}) collective-permute-start(bf16[1,1024,512]{1,2,0:T(8,128)(2,1)S(1)} %bitcast.243), channel_id=1, source_target_pairs={{1,0},{2,1},{3,2},{5,4},{6,5},{7,6},{9,8},{10,9},{11,10},{13,12},{... | collective-permute-start | bytes 3145736 | tf_op jit(solution)/shard_map/ppermute | solution.py:16
  (18 other events, 40.1 us)
Sparse Core Ops, SparseCore 0:
  295.9 159.4 reduce-scatter.1
where the time goes:
time: 465 us; the launch traced here: 462 us
  matrix products  215 us (46%)
  waiting for transfers between devices  153 us (33%)
  local copies, waits for them, and re-layouts  50.2 us (11%)
  other arithmetic  17.7 us (4%)
  between operations  14.5 us (3%)
  starting transfers between devices  10.9 us (2%)
    reduce_scatter x1, waiting for transfers between devices, on_device(): lax.psum_scatter(local_grads, ('dp', 'tm'), scatter_dimension=0, tiled=True)  153 us
    dot_general x16, matrix products, per_head(): jnp.dot(query_rows, key_rows.T, preferred_element_type=jnp.float32)  65 us
    dot_general x16, matrix products, per_head(): jnp.dot(grad_rows, value_rows.T, preferred_element_type=jnp.float32)  44 us
    dot_general x16, matrix products, per_head(): jnp.dot(score_grad.T, query_rows, preferred_element_type=jnp.float32)  33.6 us
    dot_general x16, matrix products, per_head(): jnp.dot(score_grad, key_rows, preferred_element_type=jnp.float32)  30.4 us
    dot_general x16, matrix products, per_head(): jnp.dot(weights_low.T, grad_rows, preferred_element_type=jnp.float32)  19.1 us
    dynamic_slice x48, local copies, waits for them, and re-layouts, block_grads(): lax.map(per_head, (query_heads, key_heads, value_heads, grad_heads, saved...  15.5 us
    reshape x6, local copies, waits for them, and re-layouts, split_heads(): return matrix.reshape(matrix.shape[0], HEADS, HEAD_DIM).transpose(1, 0, 2)  14.5 us
  transfers between devices with their start and end apart: 5, of which 1 were waited for; matrix products, arithmetic and copies ran while one was open for 8% of the time, Pallas kernels for 0%

commit v1 on v0

v1 whole, which is shorter than its diff:
```python
import functools
import math

import jax
import jax.numpy as jnp
from jax import lax
from jax.experimental import pallas as pl
from jax.experimental.pallas import tpu as pltpu
from jax.sharding import PartitionSpec as P

HEADS = 8
HEAD_DIM = 64
TILE = 256
SCALE = HEAD_DIM**-0.5
LOG2E = math.log2(math.e)
LN2 = math.log(2.0)
F32 = jnp.float32
BF16 = jnp.bfloat16
VMEM = pl.BlockSpec(memory_space=pltpu.VMEM)


def mm(a, b, ca, cb):
    return lax.dot_general(a, b, (((ca,), (cb,)), ((), ())), preferred_element_type=F32)


def twice(x):
    return jnp.concatenate([x, x], axis=1)


def half_mask(h):
    lane = lax.broadcasted_iota(jnp.int32, (1, 128), 1)
    return lane < HEAD_DIM if h == 0 else lane >= HEAD_DIM


def attention(near, refs, scratch, put_query, put_key, put_value):
    q_ref, do_ref, qt_ref, dot_ref, k_ref, v_ref, aux_ref = refs
    km, vm, lseb, offb, prob, grad, acc = scratch
    bins = q_ref.shape[0]
    blocks = bins // TILE

    def body(pair, carry):
        base = pl.multiple_of(pair * 128, 128)
        cols = pl.ds(base, 128)
        for h in range(2):
            rows = pl.ds(pl.multiple_of(base + h * HEAD_DIM, HEAD_DIM), HEAD_DIM)
            mask = half_mask(h)
            k2, v2 = k_ref[:, cols], v_ref[:, cols]
            km[h] = jnp.where(mask, k2, jnp.zeros_like(k2))
            vm[h] = jnp.where(mask, v2, jnp.zeros_like(v2))
            lane = lax.broadcasted_iota(jnp.int32, (1, 128), 1)
            aux = aux_ref[...]
            head = pair * 2 + h
            lse = jnp.sum(jnp.where(lane == head, aux, 0.0), axis=1, keepdims=True)
            off = jnp.sum(jnp.where(lane == head + HEADS, aux, 0.0), axis=1, keepdims=True)
            lseb[...] = jnp.broadcast_to(lse, (bins, 128))
            offb[...] = jnp.broadcast_to(off, (bins, 128))
            for j in range(blocks):
                ks = slice(j * TILE, (j + 1) * TILE)
                kw, vw = km[h, ks, :], vm[h, ks, :]
                for i in range(j, blocks) if near else range(j + 1):
                    qs = slice(i * TILE, (i + 1) * TILE)
                    p = jnp.exp2(mm(q_ref[qs, cols], kw, 1, 1) - twice(lseb[qs, :]))
                    if i == j:
                        r = lax.broadcasted_iota(jnp.int32, (TILE, TILE), 0)
                        c = lax.broadcasted_iota(jnp.int32, (TILE, TILE), 1)
                        p = jnp.where(r >= c if near else r < c, p, 0.0)
                    dp = mm(do_ref[qs, cols], vw, 1, 1)
                    prob[h, qs, ks] = p.astype(BF16)
                    grad[h, qs, ks] = (p * (dp - twice(offb[qs, :]))).astype(BF16)
            for j in range(blocks):
                ks = slice(j * TILE, (j + 1) * TILE)
                qs = slice(j * TILE, bins) if near else slice(0, (j + 1) * TILE)
                put_value(rows, ks, mm(dot_ref[rows, qs], prob[h, qs, ks], 1, 0))
                put_key(rows, ks, mm(qt_ref[rows, qs], grad[h, qs, ks], 1, 0) * LN2)
            for i in range(blocks):
                qs = slice(i * TILE, (i + 1) * TILE)
                ks = slice(0, (i + 1) * TILE) if near else slice(i * TILE, bins)
                part = mm(grad[h, qs, ks], km[h, ks, :], 1, 0)
                if h == 0:
                    acc[qs, :] = part
                else:
                    put_query(qs, cols, (acc[qs, :] + part) * SCALE)
        return carry

    lax.fori_loop(0, HEADS // 2, body, 0)


def attention_scratch(bins):
    return [
        pltpu.VMEM((2, bins, 128), BF16),
        pltpu.VMEM((2, bins, 128), BF16),
        pltpu.VMEM((bins, 128), F32),
        pltpu.VMEM((bins, 128), F32),
        pltpu.VMEM((2, bins, bins), BF16),
        pltpu.VMEM((2, bins, bins), BF16),
        pltpu.VMEM((bins, 128), F32),
    ]


def near_kernel(
    x_ref, wq_ref, wk_ref, wv_ref, wo_ref, saved_ref, up_ref, lse_ref,
    q_ref, do_ref, qt_ref, dot_ref, aux_ref, dq_ref, dkt_ref, dvt_ref, gwo_ref,
    k_ref, v_ref, *scratch,
):
    bins, width = x_ref.shape
    for b in range(bins // TILE):
        bs = slice(b * TILE, (b + 1) * TILE)
        x = x_ref[bs, :]
        q = (mm(x, wq_ref[...], 1, 0) * (SCALE * LOG2E)).astype(BF16)
        q_ref[bs, :] = q
        qt_ref[:, bs] = q.T
        k_ref[bs, :] = mm(x, wk_ref[...], 1, 0).astype(BF16)
        v_ref[bs, :] = mm(x, wv_ref[...], 1, 0).astype(BF16)
        do = mm(up_ref[bs, :], wo_ref[...], 1, 1).astype(BF16)
        do_ref[bs, :] = do
        dot_ref[:, bs] = do.T
        prod = do.astype(F32) * saved_ref[bs, :].astype(F32)
        lane = lax.broadcasted_iota(jnp.int32, (1, 128), 1)
        padded = jnp.concatenate([lse_ref[:, bs] * LOG2E, jnp.zeros((128 - HEADS, TILE), F32)], axis=0)
        aux = padded.T
        for head in range(HEADS):
            slab = prod[:, head // 2 * 128 : head // 2 * 128 + 128]
            off = jnp.sum(jnp.where(half_mask(head % 2), slab, 0.0), axis=1, keepdims=True)
            aux = jnp.where(lane == HEADS + head, off, aux)
        aux_ref[bs, :] = aux
    gwo_ref[...] = mm(saved_ref[...], up_ref[...], 0, 0).astype(BF16)

    def put_query(qs, cols, value):
        dq_ref[qs, cols] = value

    def put_key(rows, ks, value):
        dkt_ref[rows, ks] = value.astype(BF16)

    def put_value(rows, ks, value):
        dvt_ref[rows, ks] = value.astype(BF16)

    attention(
        True, (q_ref, do_ref, qt_ref, dot_ref, k_ref, v_ref, aux_ref), scratch, put_query, put_key, put_value
    )


def far_kernel(
    x_ref, xp_ref, wk_ref, wv_ref, q_ref, do_ref, qt_ref, dot_ref, aux_ref, dqn_ref, dkt_ref, dvt_ref,
    dq_ref, back_ref, gw_ref,
    k_ref, v_ref, dkf, dvf, xt, xpt, *scratch,
):
    bins, width = x_ref.shape
    for b in range(bins // TILE):
        bs = slice(b * TILE, (b + 1) * TILE)
        xp = xp_ref[bs, :]
        k_ref[bs, :] = mm(xp, wk_ref[...], 1, 0).astype(BF16)
        v_ref[bs, :] = mm(xp, wv_ref[...], 1, 0).astype(BF16)
        xpt[:, bs] = xp.T
        xt[:, bs] = x_ref[bs, :].T

    def put_query(qs, cols, value):
        dq_ref[qs, cols] = (dqn_ref[qs, cols] + value).astype(BF16)

    def put_key(rows, ks, value):
        dkf[rows, ks] = value.astype(BF16)

    def put_value(rows, ks, value):
        dvf[rows, ks] = value.astype(BF16)

    attention(
        False, (q_ref, do_ref, qt_ref, dot_ref, k_ref, v_ref, aux_ref), scratch, put_query, put_key, put_value
    )
    back_ref[...] = (mm(wk_ref[...], dkf[...], 1, 0) + mm(wv_ref[...], dvf[...], 1, 0)).astype(BF16)
    gw_ref[0:width, :] = mm(xt[...], dq_ref[...], 1, 0).astype(BF16)
    gw_ref[width : 2 * width, :] = (mm(xt[...], dkt_ref[...], 1, 1) + mm(xpt[...], dkf[...], 1, 1)).astype(BF16)
    gw_ref[2 * width :, :] = (mm(xt[...], dvt_ref[...], 1, 1) + mm(xpt[...], dvf[...], 1, 1)).astype(BF16)


def input_kernel(dq_ref, dkt_ref, dvt_ref, wq_ref, wk_ref, wv_ref, out_ref):
    out_ref[...] = (
        mm(wq_ref[...], dq_ref[...], 1, 1) + mm(wk_ref[...], dkt_ref[...], 1, 0) + mm(wv_ref[...], dvt_ref[...], 1, 0)
    )


def call(kernel, outs, scratch, flops, *args):
    return pl.pallas_call(
        kernel,
        out_shape=[jax.ShapeDtypeStruct(*o) for o in outs],
        in_specs=[VMEM] * len(args),
        out_specs=[VMEM] * len(outs),
        scratch_shapes=scratch,
        compiler_params=pltpu.CompilerParams(vmem_limit_bytes=48 * 2**20),
        cost_estimate=pl.CostEstimate(
            flops=int(flops), bytes_accessed=sum(a.size * a.dtype.itemsize for a in args), transcendentals=0
        ),
    )(*args)


def scatter_sum(parts, axes):
    me = lax.axis_index(axes)
    count = lax.axis_size(axes)
    keep = parts.astype(F32)
    step = 1
    while step < count:
        halves = keep.reshape(keep.shape[0] // 2, 2, *keep.shape[1:])
        bit = (me // step) % 2
        send = lax.dynamic_index_in_dim(halves, 1 - bit, 1, keepdims=False).astype(BF16)
        keep = lax.dynamic_index_in_dim(halves, bit, 1, keepdims=False)
        got = lax.ppermute(send, axes, [(d, d ^ step) for d in range(count)])
        keep = keep + got.astype(F32)
        step *= 2
    return keep[0]


def on_device(inputs, w_query, w_key, w_value, w_out, saved_heads, log_totals, out_grad):
    x, saved, lse, up = inputs[0], saved_heads[0], log_totals[0], out_grad[0]
    bins, width = x.shape
    tm = lax.axis_size("tm")
    x_prev = lax.ppermute(x, "tm", [(s, s + 1) for s in range(tm - 1)])
    tall, wide, square = (bins, width), (width, bins), (width, width)
    pair = 2 * HEADS * bins * bins * HEAD_DIM * 5
    q, do, qt, dot, aux, dqn, dkt, dvt, gwo = call(
        near_kernel,
        [(tall, BF16), (tall, BF16), (wide, BF16), (wide, BF16), ((bins, 128), F32), (tall, F32), (wide, BF16), (wide, BF16), (square, BF16)],
        [pltpu.VMEM(tall, BF16), pltpu.VMEM(tall, BF16)] + attention_scratch(bins),
        pair,
        x, w_query, w_key, w_value, w_out, saved, up, lse,
    )
    dq, back, gw = call(
        far_kernel,
        [(tall, BF16), (wide, BF16), ((3 * width, width), BF16)],
        [pltpu.VMEM(tall, BF16), pltpu.VMEM(tall, BF16)]
        + [pltpu.VMEM(wide, BF16)] * 4
        + attention_scratch(bins),
        pair,
        x, x_prev, w_key, w_value, q, do, qt, dot, aux, dqn, dkt, dvt,
    )
    back = lax.ppermute(back, "tm", [(s + 1, s) for s in range(tm - 1)])
    (near_grad,) = call(input_kernel, [(wide, F32)], [], 3 * 2 * bins * width * width, dq, dkt, dvt, w_query, w_key, w_value)
    axes = ("dp", "tm")
    count = lax.axis_size(axes)
    parts = jnp.concatenate([gw, gwo], axis=0).reshape(count, 4 * width // count, width)
    weight_grads = scatter_sum(parts, axes)
    input_grad = (near_grad + back.astype(F32)).T.astype(BF16)
    return input_grad[None], weight_grads


def solution(mesh):
    rows, copied = P("dp", "tm", None), P()
    return jax.shard_map(
        on_device,
        mesh=mesh,
        in_specs=(rows, copied, copied, copied, copied, rows, P("dp", None, "tm"), rows),
        out_specs=(rows, P(("dp", "tm"), None)),
        check_vma=False,
    )
```

time: 465 us -> 109 us (0.23)
  matrix products: 215 us -> 0 us
  waiting for transfers between devices: 153 us -> 21.6 us
  Pallas kernels: 0 us -> 45.5 us
  local copies, waits for them, and re-layouts: 50.2 us -> 17.5 us
  between operations: 14.5 us -> 0.89 us
  other arithmetic: 17.7 us -> 9.98 us
    dot_general x95 -> x0, matrix products: 215 us -> none  [the longest x16 65 us: per_head(): jnp.dot(query_rows, key_rows.T, preferred_element_type=jnp.float32)]
    reduce_scatter x1 -> x0, waiting for transfers between devices: 153 us -> none  [on_device(): lax.psum_scatter(local_grads, ('dp', 'tm'), scatter_dimension=0, tiled=True)]
    pallas_call x0 -> x3, Pallas kernels: none -> 45.5 us  [call(): pl.pallas_call(kernel, out_shape=[jax.ShapeDtypeStruct(*o) for o in outs]...]
    ppermute x4 -> x7, waiting for transfers between devices: 0.01 us -> 21.6 us  [the longest x5 21.6 us: scatter_sum(): got = lax.ppermute(send, axes, [(d, d ^ step) for d in range(count)])]
    dynamic_slice x48 -> x0, local copies, waits for them, and re-layouts: 15.5 us -> none  [block_grads(): lax.map(per_head, (query_heads, key_heads, value_heads, grad_heads, saved...]
    reshape x6 -> x0, local copies, waits for them, and re-layouts: 14.5 us -> none  [split_heads(): return matrix.reshape(matrix.shape[0], HEADS, HEAD_DIM).transpose(1, 0, 2)]
    unnamed x43 -> x37, local copies, waits for them, and re-layouts: 5.03 us -> 15.7 us
    concatenate x2 -> x1, other arithmetic: 11.2 us -> 1.92 us  [on_device(): jnp.concatenate([gw, gwo], axis=0).reshape(count, 4 * width // count, width)]
  transfers between devices with their start and end apart: 5 -> 7, of which waited for: 1 -> 3; matrix products, arithmetic and copies ran while one was open for 8% -> 4% of each run, Pallas kernels for 0% -> 21%
where the time goes in v1:
time: 109 us; the launch traced here: 108 us
  Pallas kernels  45.5 us (42%)
  waiting for transfers between devices  21.6 us (20%)
  local copies, waits for them, and re-layouts  17.5 us (16%)
  starting transfers between devices  12.4 us (11%)
  other arithmetic  9.98 us (9%)
    pallas_call x3, Pallas kernels, call(): pl.pallas_call(kernel, out_shape=[jax.ShapeDtypeStruct(*o) for o in outs]...  45.5 us
    ppermute x5, waiting for transfers between devices, scatter_sum(): got = lax.ppermute(send, axes, [(d, d ^ step) for d in range(count)])  21.6 us
    unnamed x37, local copies, waits for them, and re-layouts  15.7 us
    ppermute x5, starting transfers between devices, scatter_sum(): got = lax.ppermute(send, axes, [(d, d ^ step) for d in range(count)])  8.67 us
    add x4, other arithmetic, scatter_sum(): keep = keep + got.astype(F32)  4.63 us
    ppermute x1, starting transfers between devices, on_device(): x_prev = lax.ppermute(x, 'tm', [(s, s + 1) for s in range(tm - 1)])  2.46 us
    broadcast_in_dim x1, other arithmetic, on_device(): return (input_grad[None], weight_grads)  2.2 us
  transfers between devices with their start and end apart: 7, of which 3 were waited for; matrix products, arithmetic and copies ran while one was open for 4% of the time, Pallas kernels for 21%

profile of v1, /device:TPU:0, one launch (start us, length us, event | category | flops | bytes accessed | tf_op | source)
XLA Modules:
  0.0 107.9 jit_solution(1196459902400712425)
XLA Ops:
  0.6 2.5 %collective-permute-start = (bf16[1024,512]{1,0:T(8,128)(2,1)}, bf16[1024,512]{1,0:T(8,128)(2,1)S(1)}, u32[]{:S(2)}, u32[]{:S(2)}) collective-permute-start(bf16[1024,512]{1,0:T(8,128)(2,1)} %bitcast.35), channel_id=1, source_target_pairs={{0,1},{1,2},{2,3},{4,5},{5,6},{6,7},{8,9},{9,10},{10,11},{12,13},{... | collective-permute-start | bytes 3145736 | tf_op jit(solution)/shard_map/ppermute | solution.py:214
  4.2 1.0 copy-done.5
  5.2 1.0 copy-done.7
  8.1 19.8 %shard_map.95 = (bf16[1024,512]{1,0:T(8,128)(2,1)S(1)}, bf16[1024,512]{1,0:T(8,128)(2,1)S(1)}, bf16[512,1024]{1,0:T(8,128)(2,1)}, bf16[512,1024]{1,0:T(8,128)(2,...) custom-call(bf16[1024,512]{1,0:T(8,128)(2,1)} %bitcast.36, ...), custom_call_target="tpu_custom_call" | custom-call | flops 5368709120 | bytes 5275648 | tf_op jit(solution)/shard_map/pallas_call | solution.py:181
  28.8 1.0 copy-done.14
  29.9 22.6 %shard_map.96 = (bf16[1024,512]{1,0:T(8,128)(2,1)S(1)}, bf16[512,1024]{1,0:T(8,128)(2,1)S(1)}, bf16[1536,512]{1,0:T(8,128)(2,1)}) custom-call(bf16[1024,512]{1,0:T(8,128)(2,1)S(1)} %bitcast.37, bf16[1024,512]{1,0:T(8,128)(2,1)S(1)} %collective-permute-done.xp_ref, bf16[512,512]{1,0:T(8,128)(2,1)S(1)} %copy-done.3, bf16[512,512]{1,0:T(8,128)(2,1)S(1)} %copy-done.5, ...), custom_call_target="tpu_custom_call" | custom-call | flops 5368709120 | bytes 12058624 | tf_op jit(solution)/shard_map/pallas_call | solution.py:181
  52.5 1.9 %pad_maximum_fusion = bf16[2048,512]{1,0:T(8,128)(2,1)S(1)} fusion(bf16[512,512]{1,0:T(8,128)(2,1)S(1)} %get-tuple-element.25, bf16[1536,512]{1,0:T(8,128)(2,1)} %get-tuple-element.24), kind=kLoop, calls=%fused_computation | loop fusion | flops 4194304 | bytes 4194304 | tf_op jit(solution)/shard_map/concatenate | solution.py:237
  55.0 2.0 %copy-done.15 = f32[16,2,64,512]{3,2,1,0:T(8,128)} copy-done((f32[16,2,64,512]{3,2,1,0:T(8,128)}, f32[16,2,64,512]{3,2,1,0:T(8,128)S(1)}, u32[]{:S(2)}) %copy-start.15) | copy-done | bytes 4194328
  57.2 2.6 %collective-permute-start.2 = (bf16[16,64,512]{2,1,0:T(8,128)(2,1)S(1)}, bf16[16,64,512]{2,1,0:T(8,128)(2,1)S(1)}, u32[]{:S(2)}, u32[]{:S(2)}) collective-permute-start(bf16[16,64,512]{2,1,0:T(8,128)(2,1)S(1)} %fusion.1), channel_id=1, source_target_pairs={{0,1},{1,0},{2,3},{3,2},{4,5},{5,4},{6,7},{7,6},{8,9},{9,8},{10,11... | collective-permute-start | bytes 3145736 | tf_op jit(solution)/shard_map/ppermute | solution.py:204
  59.8 2.3 %collective-permute-done.2 = bf16[16,64,512]{2,1,0:T(8,128)(2,1)S(1)} collective-permute-done((bf16[16,64,512]{2,1,0:T(8,128)(2,1)S(1)}, bf16[16,64,512]{2,1,0:T(8,128)(2,1)S(1)}, u32[]{:S(2)}, u32[]{:S(2)}) %collective-permute-start.2) | collective-permute-done | bytes 1048608 | tf_op jit(solution)/shard_map/ppermute | solution.py:204
  62.0 1.9 %bitcast_add_fusion = f32[16,64,512]{2,1,0:T(8,128)S(1)} fusion(bf16[16,64,512]{2,1,0:T(8,128)(2,1)S(1)} %collective-permute-done.2, f32[16,2,64,512]{3,2,1,0:T(8,128)} %copy-done.15, s32[]{:T(128)S(6)} %select_n.73), kind=kLoop, calls=%fused_computation.2 | loop fusion | flops 1048576 | bytes 5242884 | tf_op jit(solution)/shard_map/add | solution.py:205
  64.0 1.3 %copy-done.16 = f32[16,64,512]{2,1,0:T(8,128)} copy-done((f32[16,64,512]{2,1,0:T(8,128)}, f32[16,64,512]{2,1,0:T(8,128)S(1)}, u32[]{:S(2)}) %copy-start.16) | copy-done | bytes 2097176
  66.4 14.2 %collective-permute-done.3 = bf16[8,64,512]{2,1,0:T(8,128)(2,1)} collective-permute-done((bf16[8,64,512]{2,1,0:T(8,128)(2,1)}, bf16[8,64,512]{2,1,0:T(8,128)(2,1)}, u32[]{:S(2)}, u32[]{:S(2)}) %collective-permute-start.3) | collective-permute-done | bytes 524320 | tf_op jit(solution)/shard_map/ppermute | solution.py:204
  80.7 1.6 %bitcast_add_fusion.1 = f32[8,64,512]{2,1,0:T(8,128)S(1)} fusion(bf16[8,64,512]{2,1,0:T(8,128)(2,1)} %collective-permute-done.3, f32[8,2,64,512]{3,2,1,0:T(8,128)} %bitcast.41, s32[]{:T(128)S(6)} %select_n.77), kind=kLoop, calls=%fused_computation.6 | loop fusion | flops 524288 | bytes 2621444 | tf_op jit(solution)/shard_map/add | solution.py:205
  83.9 1.5 %collective-permute-start.4 = (bf16[4,64,512]{2,1,0:T(8,128)(2,1)}, bf16[4,64,512]{2,1,0:T(8,128)(2,1)S(1)}, u32[]{:S(2)}, u32[]{:S(2)}) collective-permute-start(bf16[4,64,512]{2,1,0:T(8,128)(2,1)} %fusion.3), channel_id=1, source_target_pairs={{0,4},{1,5},{2,6},{3,7},{4,0},{5,1},{6,2},{7,3},{8,12},{9,13},{10,... | collective-permute-start | bytes 786440 | tf_op jit(solution)/shard_map/ppermute | solution.py:204
  85.5 1.3 %collective-permute-start.1 = (bf16[512,1024]{1,0:T(8,128)(2,1)}, bf16[512,1024]{1,0:T(8,128)(2,1)}, u32[]{:S(2)}, u32[]{:S(2)}) collective-permute-start(bf16[512,1024]{1,0:T(8,128)(2,1)} %copy-done.10), channel_id=1, source_target_pairs={{1,0},{2,1},{3,2},{5,4},{6,5},{7,6},{9,8},{10,9},{11,10},{13,12},{... | collective-permute-start | bytes 3145736 | tf_op jit(solution)/shard_map/ppermute | solution.py:233
  86.8 5.1 %collective-permute-done.4 = bf16[4,64,512]{2,1,0:T(8,128)(2,1)S(1)} collective-permute-done((bf16[4,64,512]{2,1,0:T(8,128)(2,1)}, bf16[4,64,512]{2,1,0:T(8,128)(2,1)S(1)}, u32[]{:S(2)}, u32[]{:S(2)}) %collective-permute-start.4) | collective-permute-done | bytes 262176 | tf_op jit(solution)/shard_map/ppermute | solution.py:204
  91.9 1.1 %bitcast_add_fusion.2 = f32[4,64,512]{2,1,0:T(8,128)S(1)} fusion(bf16[4,64,512]{2,1,0:T(8,128)(2,1)S(1)} %collective-permute-done.4, f32[4,2,64,512]{3,2,1,0:T(8,128)} %bitcast.43, s32[]{:T(128)S(6)} %select_n.81), kind=kLoop, calls=%fused_computation.9 | loop fusion | flops 262144 | bytes 1310724 | tf_op jit(solution)/shard_map/add | solution.py:205
  93.0 1.6 %collective-permute-start.5 = (bf16[2,64,512]{2,1,0:T(8,128)(2,1)S(1)}, bf16[2,64,512]{2,1,0:T(8,128)(2,1)S(1)}, u32[]{:S(2)}, u32[]{:S(2)}) collective-permute-start(bf16[2,64,512]{2,1,0:T(8,128)(2,1)S(1)} %fusion.4), channel_id=1, source_target_pairs={{0,8},{1,9},{2,10},{3,11},{4,12},{5,13},{6,14},{7,15},{8,0},{9,1},... | collective-permute-start | bytes 393224 | tf_op jit(solution)/shard_map/ppermute | solution.py:204
  94.7 1.0 copy-done.4
  97.8 3.1 %shard_map.97 = f32[512,1024]{1,0:T(8,128)} custom-call(bf16[1024,512]{1,0:T(8,128)(2,1)S(1)} %get-tuple-element.22.dq_ref, bf16[512,1024]{1,0:T(8,128)(2,1)S(1)} %copy-done, bf16[512,1024]{1,0:T(8,128)(2,1)S(1)} %copy-done.1, bf16[512,512]{1,0:T(8,128)(2,1)S(1)} %copy-done.8, bf16[512,512]{1,0:T(8,128)(2,1)S(1)} %copy-done.4, bf16[512,512]{1,0:T(8,128)(2,1)S(1)} %copy-done.6), custom_call_target="tpu_custom_call" | custom-call | flops 1610612736 | bytes 4718592 | tf_op jit(solution)/shard_map/pallas_call | solution.py:181
  101.0 2.7 %collective-permute-start.6 = (bf16[1,64,512]{2,1,0:T(8,128)(2,1)S(1)}, bf16[1,64,512]{2,1,0:T(8,128)(2,1)S(1)}, u32[]{:S(2)}, u32[]{:S(2)}) collective-permute-start(bf16[1,64,512]{2,1,0:T(8,128)(2,1)S(1)} %dynamic-slice_convert_fusion.3), channel_id=1, source_target_pairs={{0,16},{1,17},{2,18},{3,19},{4,20},{5,21},{6,22},{7,23},{8,24},{9,... | collective-permute-start | bytes 196616 | tf_op jit(solution)/shard_map/ppermute | solution.py:204
  103.6 2.2 %fusion = bf16[1,1024,512]{1,2,0:T(8,128)(2,1)S(1)} fusion(f32[512,1024]{1,0:T(8,128)} %shard_map.97, bf16[512,1024]{1,0:T(8,128)(2,1)} %collective-permute-done.1), kind=kLoop, calls=%fused_computation.4 | loop fusion | flops 1572864 | bytes 4194304 | tf_op jit(solution)/shard_map/broadcast_in_dim | solution.py:240
  105.9 1.3 %copy.14 = bf16[1,1024,512]{2,1,0:T(8,128)(2,1)} copy(bf16[1,1024,512]{1,2,0:T(8,128)(2,1)S(1)} %fusion) | data formatting | bytes 2097152
  (43 shorter events, 10.2 us)
Async XLA Ops:
  0.6 29.2 %collective-permute-start = (bf16[1024,512]{1,0:T(8,128)(2,1)}, bf16[1024,512]{1,0:T(8,128)(2,1)S(1)}, u32[]{:S(2)}, u32[]{:S(2)}) collective-permute-start(bf16[1024,512]{1,0:T(8,128)(2,1)} %bitcast.35), channel_id=1, source_target_pairs={{0,1},{1,2},{2,3},{4,5},{5,6},{6,7},{8,9},{9,10},{10,11},{12,13},{... | collective-permute-start | bytes 3145736 | tf_op jit(solution)/shard_map/ppermute | solution.py:214
  3.1 1.0 copy-start.2
  4.2 1.0 copy-start.5
  5.2 1.0 copy-start.7
  6.3 1.0 copy-start.11
  8.1 21.8 %copy-start.3 = (bf16[512,512]{1,0:T(8,128)(2,1)S(1)}, bf16[512,512]{1,0:T(8,128)(2,1)}, u32[]{:S(2)}) copy-start(bf16[512,512]{1,0:T(8,128)(2,1)} %wk_ref.5) | copy-start | bytes 1572868
  8.1 21.8 %copy-start.9 = (bf16[1,1024,512]{2,1,0:T(8,128)(2,1)S(1)}, bf16[1,1024,512]{2,1,0:T(8,128)(2,1)}, u32[]{:S(2)}) copy-start(bf16[1,1024,512]{2,1,0:T(8,128)(2,1)} %param.8) | copy-start | bytes 3145732
  27.8 1.0 copy-start.13
  28.8 1.0 copy-start.14
  52.5 1.9 %copy-start.10 = (bf16[512,1024]{1,0:T(8,128)(2,1)}, bf16[512,1024]{1,0:T(8,128)(2,1)S(1)}, u32[]{:S(2)}) copy-start(bf16[512,1024]{1,0:T(8,128)(2,1)S(1)} %get-tuple-element.23) | copy-start | bytes 3145732
  55.0 2.0 %copy-start.15 = (f32[16,2,64,512]{3,2,1,0:T(8,128)}, f32[16,2,64,512]{3,2,1,0:T(8,128)S(1)}, u32[]{:S(2)}) copy-start(f32[16,2,64,512]{3,2,1,0:T(8,128)S(1)} %convert.1) | copy-start | bytes 12582916
  57.2 4.9 %collective-permute-start.2 = (bf16[16,64,512]{2,1,0:T(8,128)(2,1)S(1)}, bf16[16,64,512]{2,1,0:T(8,128)(2,1)S(1)}, u32[]{:S(2)}, u32[]{:S(2)}) collective-permute-start(bf16[16,64,512]{2,1,0:T(8,128)(2,1)S(1)} %fusion.1), channel_id=1, source_target_pairs={{0,1},{1,0},{2,3},{3,2},{4,5},{5,4},{6,7},{7,6},{8,9},{9,8},{10,11... | collective-permute-start | bytes 3145736 | tf_op jit(solution)/shard_map/ppermute | solution.py:204
  64.0 1.3 %copy-start.16 = (f32[16,64,512]{2,1,0:T(8,128)}, f32[16,64,512]{2,1,0:T(8,128)S(1)}, u32[]{:S(2)}) copy-start(f32[16,64,512]{2,1,0:T(8,128)S(1)} %bitcast_add_fusion) | copy-start | bytes 6291460
  66.1 14.5 %collective-permute-start.3 = (bf16[8,64,512]{2,1,0:T(8,128)(2,1)}, bf16[8,64,512]{2,1,0:T(8,128)(2,1)}, u32[]{:S(2)}, u32[]{:S(2)}) collective-permute-start(bf16[8,64,512]{2,1,0:T(8,128)(2,1)} %fusion.2), channel_id=1, source_target_pairs={{0,2},{1,3},{2,0},{3,1},{4,6},{5,7},{6,4},{7,5},{8,10},{9,11},{10,... | collective-permute-start | bytes 1572872 | tf_op jit(solution)/shard_map/ppermute | solution.py:204
  66.4 28.3 %copy-start = (bf16[512,1024]{1,0:T(8,128)(2,1)S(1)}, bf16[512,1024]{1,0:T(8,128)(2,1)}, u32[]{:S(2)}) copy-start(bf16[512,1024]{1,0:T(8,128)(2,1)} %get-tuple-element.20.dkt_ref) | copy-start | bytes 3145732
  66.4 28.3 %copy-start.1 = (bf16[512,1024]{1,0:T(8,128)(2,1)S(1)}, bf16[512,1024]{1,0:T(8,128)(2,1)}, u32[]{:S(2)}) copy-start(bf16[512,1024]{1,0:T(8,128)(2,1)} %get-tuple-element.21.dvt_ref) | copy-start | bytes 3145732
  82.2 1.0 copy-start.17
  83.9 7.9 %collective-permute-start.4 = (bf16[4,64,512]{2,1,0:T(8,128)(2,1)}, bf16[4,64,512]{2,1,0:T(8,128)(2,1)S(1)}, u32[]{:S(2)}, u32[]{:S(2)}) collective-permute-start(bf16[4,64,512]{2,1,0:T(8,128)(2,1)} %fusion.3), channel_id=1, source_target_pairs={{0,4},{1,5},{2,6},{3,7},{4,0},{5,1},{6,2},{7,3},{8,12},{9,13},{10,... | collective-permute-start | bytes 786440 | tf_op jit(solution)/shard_map/ppermute | solution.py:204
  85.5 18.2 %collective-permute-start.1 = (bf16[512,1024]{1,0:T(8,128)(2,1)}, bf16[512,1024]{1,0:T(8,128)(2,1)}, u32[]{:S(2)}, u32[]{:S(2)}) collective-permute-start(bf16[512,1024]{1,0:T(8,128)(2,1)} %copy-done.10), channel_id=1, source_target_pairs={{1,0},{2,1},{3,2},{5,4},{6,5},{7,6},{9,8},{10,9},{11,10},{13,12},{... | collective-permute-start | bytes 3145736 | tf_op jit(solution)/shard_map/ppermute | solution.py:233
  93.0 7.9 %collective-permute-start.5 = (bf16[2,64,512]{2,1,0:T(8,128)(2,1)S(1)}, bf16[2,64,512]{2,1,0:T(8,128)(2,1)S(1)}, u32[]{:S(2)}, u32[]{:S(2)}) collective-permute-start(bf16[2,64,512]{2,1,0:T(8,128)(2,1)S(1)} %fusion.4), channel_id=1, source_target_pairs={{0,8},{1,9},{2,10},{3,11},{4,12},{5,13},{6,14},{7,15},{8,0},{9,1},... | collective-permute-start | bytes 393224 | tf_op jit(solution)/shard_map/ppermute | solution.py:204
  94.7 1.0 copy-start.4
  95.7 1.0 copy-start.6
  96.8 1.0 copy-start.8
  101.0 6.2 %collective-permute-start.6 = (bf16[1,64,512]{2,1,0:T(8,128)(2,1)S(1)}, bf16[1,64,512]{2,1,0:T(8,128)(2,1)S(1)}, u32[]{:S(2)}, u32[]{:S(2)}) collective-permute-start(bf16[1,64,512]{2,1,0:T(8,128)(2,1)S(1)} %dynamic-slice_convert_fusion.3), channel_id=1, source_target_pairs={{0,16},{1,17},{2,18},{3,19},{4,20},{5,21},{6,22},{7,23},{8,24},{9,... | collective-permute-start | bytes 196616 | tf_op jit(solution)/shard_map/ppermute | solution.py:204
  (1 other events, 0.8 us)

commit v2 on v1

--- a/solution.py
+++ b/solution.py
@@ -98,24 +98,40 @@
 
 
 def near_kernel(
-    x_ref, wq_ref, wk_ref, wv_ref, wo_ref, saved_ref, up_ref, lse_ref,
-    q_ref, do_ref, qt_ref, dot_ref, aux_ref, dq_ref, dkt_ref, dvt_ref, gwo_ref,
-    k_ref, v_ref, *scratch,
+    x_hbm, wq_hbm, wk_hbm, wv_hbm, wo_hbm, saved_hbm, up_hbm, lse_hbm,
+    q_ref, do_ref, qt_ref, dot_ref, aux_ref, dq_ref, dkt_ref, dvt_ref, gwo_ref, xt_ref, wq_ref, wk_ref, wv_ref,
+    x_ref, wo_ref, saved_ref, up_ref, lse_ref, k_ref, v_ref, sems, *scratch,
 ):
+    sources = (up_hbm, wo_hbm, x_hbm, wq_hbm, wk_hbm, wv_hbm, saved_hbm, lse_hbm)
+    targets = (up_ref, wo_ref, x_ref, wq_ref, wk_ref, wv_ref, saved_ref, lse_ref)
+    copies = [pltpu.make_async_copy(a, b, sems.at[i]) for i, (a, b) in enumerate(zip(sources, targets))]
+    for copy in copies:
+        copy.start()
     bins, width = x_ref.shape
-    for b in range(bins // TILE):
-        bs = slice(b * TILE, (b + 1) * TILE)
-        x = x_ref[bs, :]
-        q = (mm(x, wq_ref[...], 1, 0) * (SCALE * LOG2E)).astype(BF16)
-        q_ref[bs, :] = q
-        qt_ref[:, bs] = q.T
-        k_ref[bs, :] = mm(x, wk_ref[...], 1, 0).astype(BF16)
-        v_ref[bs, :] = mm(x, wv_ref[...], 1, 0).astype(BF16)
+    tiles = [slice(b * TILE, (b + 1) * TILE) for b in range(bins // TILE)]
+    copies[0].wait()
+    copies[1].wait()
+    for bs in tiles:
         do = mm(up_ref[bs, :], wo_ref[...], 1, 1).astype(BF16)
         do_ref[bs, :] = do
         dot_ref[:, bs] = do.T
-        prod = do.astype(F32) * saved_ref[bs, :].astype(F32)
-        lane = lax.broadcasted_iota(jnp.int32, (1, 128), 1)
+    copies[2].wait()
+    copies[3].wait()
+    for bs in tiles:
+        q = (mm(x_ref[bs, :], wq_ref[...], 1, 0) * (SCALE * LOG2E)).astype(BF16)
+        q_ref[bs, :] = q
+        qt_ref[:, bs] = q.T
+        xt_ref[:, bs] = x_ref[bs, :].T
+    copies[4].wait()
+    copies[5].wait()
+    for bs in tiles:
+        k_ref[bs, :] = mm(x_ref[bs, :], wk_ref[...], 1, 0).astype(BF16)
+        v_ref[bs, :] = mm(x_ref[bs, :], wv_ref[...], 1, 0).astype(BF16)
+    copies[6].wait()
+    copies[7].wait()
+    lane = lax.broadcasted_iota(jnp.int32, (1, 128), 1)
+    for bs in tiles:
+        prod = do_ref[bs, :].astype(F32) * saved_ref[bs, :].astype(F32)
         padded = jnp.concatenate([lse_ref[:, bs] * LOG2E, jnp.zeros((128 - HEADS, TILE), F32)], axis=0)
         aux = padded.T
         for head in range(HEADS):
@@ -123,7 +139,7 @@
             off = jnp.sum(jnp.where(half_mask(head % 2), slab, 0.0), axis=1, keepdims=True)
             aux = jnp.where(lane == HEADS + head, off, aux)
         aux_ref[bs, :] = aux
-    gwo_ref[...] = mm(saved_ref[...], up_ref[...], 0, 0).astype(BF16)
+    gwo_ref[...] = mm(saved_ref[...], up_ref[...], 0, 0)
 
     def put_query(qs, cols, value):
         dq_ref[qs, cols] = value
@@ -140,18 +156,17 @@
 
 
 def far_kernel(
-    x_ref, xp_ref, wk_ref, wv_ref, q_ref, do_ref, qt_ref, dot_ref, aux_ref, dqn_ref, dkt_ref, dvt_ref,
-    dq_ref, back_ref, gw_ref,
-    k_ref, v_ref, dkf, dvf, xt, xpt, *scratch,
+    xp_ref, wk_ref, wv_ref, q_ref, do_ref, qt_ref, dot_ref, aux_ref, dqn_ref,
+    dq_ref, back_ref, dkf, dvf, xpt,
+    k_ref, v_ref, *scratch,
 ):
-    bins, width = x_ref.shape
+    bins, width = xp_ref.shape
     for b in range(bins // TILE):
         bs = slice(b * TILE, (b + 1) * TILE)
         xp = xp_ref[bs, :]
         k_ref[bs, :] = mm(xp, wk_ref[...], 1, 0).astype(BF16)
         v_ref[bs, :] = mm(xp, wv_ref[...], 1, 0).astype(BF16)
         xpt[:, bs] = xp.T
-        xt[:, bs] = x_ref[bs, :].T
 
     def put_query(qs, cols, value):
         dq_ref[qs, cols] = (dqn_ref[qs, cols] + value).astype(BF16)
@@ -166,77 +181,153 @@
         False, (q_ref, do_ref, qt_ref, dot_ref, k_ref, v_ref, aux_ref), scratch, put_query, put_key, put_value
     )
     back_ref[...] = (mm(wk_ref[...], dkf[...], 1, 0) + mm(wv_ref[...], dvf[...], 1, 0)).astype(BF16)
-    gw_ref[0:width, :] = mm(xt[...], dq_ref[...], 1, 0).astype(BF16)
-    gw_ref[width : 2 * width, :] = (mm(xt[...], dkt_ref[...], 1, 1) + mm(xpt[...], dkf[...], 1, 1)).astype(BF16)
-    gw_ref[2 * width :, :] = (mm(xt[...], dvt_ref[...], 1, 1) + mm(xpt[...], dvf[...], 1, 1)).astype(BF16)
-
-
-def input_kernel(dq_ref, dkt_ref, dvt_ref, wq_ref, wk_ref, wv_ref, out_ref):
+
+
+def bit_order(bits, parity):
+    rest = list(range(1, bits))
+    if parity and len(rest) > 1:
+        rest[0], rest[1] = rest[1], rest[0]
+    return rest
+
+
+def place(device, order):
+    return sum(((device >> bit) & 1) << (len(order) - 1 - t) for t, bit in enumerate(order))
+
+
+def weight_kernel(count, xt_ref, xpt_ref, dq_ref, dkt_ref, dvt_ref, dkf_ref, dvf_ref, gwo_ref, send_ref, keep_ref, sums):
+    width = xt_ref.shape[0]
+    sums[0:width, :] = mm(xt_ref[...], dq_ref[...], 1, 0)
+    sums[width : 2 * width, :] = mm(xt_ref[...], dkt_ref[...], 1, 1) + mm(xpt_ref[...], dkf_ref[...], 1, 1)
+    sums[2 * width : 3 * width, :] = mm(xt_ref[...], dvt_ref[...], 1, 1) + mm(xpt_ref[...], dvf_ref[...], 1, 1)
+    sums[3 * width :, :] = gwo_ref[...]
+    rows = 4 * width // count
+    bits = count.bit_length() - 1
+    mine = lax.axis_index("tm") % 2
+    for parity in range(2):
+
+        @pl.when(mine == parity)
+        def _(parity=parity):
+            for device in range(count):
+                at = place(device, bit_order(bits, device & 1))
+                block = sums[device * rows : (device + 1) * rows, :]
+                if device & 1 == parity:
+                    keep_ref[at * rows : (at + 1) * rows, :] = block
+                else:
+                    send_ref[at * rows : (at + 1) * rows, :] = block.astype(BF16)
+
+
+def halve_kernel(bit_ref, keep_ref, got_ref, send_ref, out_ref):
+    half = out_ref.shape[0]
+    bit = bit_ref[0]
+    mine = pl.ds(pl.multiple_of(bit * half, half), half)
+    other = pl.ds(pl.multiple_of((1 - bit) * half, half), half)
+    send_ref[...] = (keep_ref[other, :] + got_ref[other, :].astype(F32)).astype(BF16)
+    out_ref[...] = keep_ref[mine, :] + got_ref[mine, :].astype(F32)
+
+
+def add_kernel(keep_ref, got_ref, out_ref):
+    out_ref[...] = keep_ref[...] + got_ref[...].astype(F32)
+
+
+def near_input_kernel(dq_ref, dkt_ref, dvt_ref, wq_ref, wk_ref, wv_ref, out_ref):
     out_ref[...] = (
         mm(wq_ref[...], dq_ref[...], 1, 1) + mm(wk_ref[...], dkt_ref[...], 1, 0) + mm(wv_ref[...], dvt_ref[...], 1, 0)
     )
 
 
-def call(kernel, outs, scratch, flops, *args):
+def input_kernel(near_ref, back_ref, out_ref):
+    bins = out_ref.shape[0]
+    for b in range(bins // TILE):
+        bs = slice(b * TILE, (b + 1) * TILE)
+        out_ref[bs, :] = (near_ref[:, bs] + back_ref[:, bs].astype(F32)).T.astype(BF16)
+
+
+def call(kernel, outs, scratch, flops, *args, specs=None, limit=24):
     return pl.pallas_call(
         kernel,
-        out_shape=[jax.ShapeDtypeStruct(*o) for o in outs],
-        in_specs=[VMEM] * len(args),
+        out_shape=outs,
+        in_specs=specs or [VMEM] * len(args),
         out_specs=[VMEM] * len(outs),
         scratch_shapes=scratch,
-        compiler_params=pltpu.CompilerParams(vmem_limit_bytes=48 * 2**20),
+        compiler_params=pltpu.CompilerParams(vmem_limit_bytes=limit * 2**20),
         cost_estimate=pl.CostEstimate(
             flops=int(flops), bytes_accessed=sum(a.size * a.dtype.itemsize for a in args), transcendentals=0
         ),
     )(*args)
 
 
-def scatter_sum(parts, axes):
+def on_chip(x):
+    return pltpu.with_memory_space_constraint(x, pltpu.VMEM)
+
+
+def scatter_sum(send, keep, axes):
+    count = lax.axis_size(axes)
+    bits = count.bit_length() - 1
     me = lax.axis_index(axes)
-    count = lax.axis_size(axes)
-    keep = parts.astype(F32)
-    step = 1
-    while step < count:
-        halves = keep.reshape(keep.shape[0] // 2, 2, *keep.shape[1:])
-        bit = (me // step) % 2
-        send = lax.dynamic_index_in_dim(halves, 1 - bit, 1, keepdims=False).astype(BF16)
-        keep = lax.dynamic_index_in_dim(halves, bit, 1, keepdims=False)
-        got = lax.ppermute(send, axes, [(d, d ^ step) for d in range(count)])
-        keep = keep + got.astype(F32)
-        step *= 2
-    return keep[0]
+    odd = me % 2 == 1
+    width = keep.shape[1]
+    got = lax.ppermute(send, axes, [(d, d ^ 1) for d in range(count)])
+    for even_bit, odd_bit in zip(bit_order(bits, 0), bit_order(bits, 1)):
+        half = keep.shape[0] // 2
+        bit = jnp.where(odd, me >> odd_bit, me >> even_bit) & 1
+        send, keep = call(
+            halve_kernel,
+            [pltpu.VMEM((half, width), BF16), pltpu.VMEM((half, width), F32)],
+            [],
+            keep.size,
+            bit.reshape(1).astype(jnp.int32),
+            on_chip(keep),
+            on_chip(got),
+            specs=[pl.BlockSpec(memory_space=pltpu.SMEM), VMEM, VMEM],
+        )
+        steps = (1 << even_bit, 1 << odd_bit)
+        got = lax.ppermute(send, axes, [(d, d ^ steps[d & 1]) for d in range(count)])
+    (out,) = call(add_kernel, [jax.ShapeDtypeStruct(keep.shape, F32)], [], keep.size, on_chip(keep), on_chip(got))
+    return out
 
 
 def on_device(inputs, w_query, w_key, w_value, w_out, saved_heads, log_totals, out_grad):
     x, saved, lse, up = inputs[0], saved_heads[0], log_totals[0], out_grad[0]
     bins, width = x.shape
     tm = lax.axis_size("tm")
+    axes = ("dp", "tm")
+    count = lax.axis_size(axes)
     x_prev = lax.ppermute(x, "tm", [(s, s + 1) for s in range(tm - 1)])
     tall, wide, square = (bins, width), (width, bins), (width, width)
-    pair = 2 * HEADS * bins * bins * HEAD_DIM * 5
-    q, do, qt, dot, aux, dqn, dkt, dvt, gwo = call(
+    one = 2 * bins * width * width
+    band = 2 * HEADS * bins * bins * HEAD_DIM * 5
+    q, do, qt, dot, aux, dqn, dkt, dvt, gwo, xt, wq, wk, wv = call(
         near_kernel,
-        [(tall, BF16), (tall, BF16), (wide, BF16), (wide, BF16), ((bins, 128), F32), (tall, F32), (wide, BF16), (wide, BF16), (square, BF16)],
+        [pltpu.VMEM(s, d) for s, d in (
+            (tall, BF16), (tall, BF16), (wide, BF16), (wide, BF16), ((bins, 128), F32), (tall, F32), (wide, BF16),
+            (wide, BF16), (square, F32), (wide, BF16), (square, BF16), (square, BF16), (square, BF16),
+        )],
+        [pltpu.VMEM(s, d) for s, d in (
+            (tall, BF16), (square, BF16), (tall, BF16), (tall, BF16), ((HEADS, bins), F32), (tall, BF16), (tall, BF16),
+        )] + [pltpu.SemaphoreType.DMA((8,))] + attention_scratch(bins),
+        band,
+        x, w_query, w_key, w_value, w_out, saved, up, lse,
+        specs=[pl.BlockSpec(memory_space=pltpu.HBM)] * 8,
+    )
+    dq, back, dkf, dvf, xpt = call(
+        far_kernel,
+        [pltpu.VMEM(s, BF16) for s in (tall, wide, wide, wide, wide)],
         [pltpu.VMEM(tall, BF16), pltpu.VMEM(tall, BF16)] + attention_scratch(bins),
-        pair,
-        x, w_query, w_key, w_value, w_out, saved, up, lse,
-    )
-    dq, back, gw = call(
-        far_kernel,
-        [(tall, BF16), (wide, BF16), ((3 * width, width), BF16)],
-        [pltpu.VMEM(tall, BF16), pltpu.VMEM(tall, BF16)]
-        + [pltpu.VMEM(wide, BF16)] * 4
-        + attention_scratch(bins),
-        pair,
-        x, x_prev, w_key, w_value, q, do, qt, dot, aux, dqn, dkt, dvt,
+        band,
+        on_chip(x_prev), wk, wv, q, do, qt, dot, aux, dqn,
     )
     back = lax.ppermute(back, "tm", [(s + 1, s) for s in range(tm - 1)])
-    (near_grad,) = call(input_kernel, [(wide, F32)], [], 3 * 2 * bins * width * width, dq, dkt, dvt, w_query, w_key, w_value)
-    axes = ("dp", "tm")
-    count = lax.axis_size(axes)
-    parts = jnp.concatenate([gw, gwo], axis=0).reshape(count, 4 * width // count, width)
-    weight_grads = scatter_sum(parts, axes)
-    input_grad = (near_grad + back.astype(F32)).T.astype(BF16)
+    half = (2 * width, width)
+    send, keep = call(
+        functools.partial(weight_kernel, count),
+        [pltpu.VMEM(half, BF16), pltpu.VMEM(half, F32)],
+        [pltpu.VMEM((4 * width, width), F32)],
+        5 * one,
+        xt, xpt, dq, dkt, dvt, dkf, dvf, gwo,
+    )
+    weight_grads = scatter_sum(send, keep, axes)
+    (near_grad,) = call(near_input_kernel, [pltpu.VMEM(wide, F32)], [], 3 * one, dq, dkt, dvt, wq, wk, wv)
+    (input_grad,) = call(input_kernel, [jax.ShapeDtypeStruct(tall, BF16)], [], one // 8, near_grad, on_chip(back))
     return input_grad[None], weight_grads
 
 

time: 109 us -> 94.7 us (0.87)
  other arithmetic: 9.98 us -> 0 us
  Pallas kernels: 45.5 us -> 43.3 us
  waiting for transfers between devices: 21.6 us -> 19.8 us
    add x4 -> x0, other arithmetic: 4.63 us -> none  [scatter_sum(): keep = keep + got.astype(F32)]
    pallas_call x3 -> x10, Pallas kernels: 45.5 us -> 43.3 us  [call(): pl.pallas_call(kernel, out_shape=outs, in_specs=specs or [VMEM] * len(arg...]
    broadcast_in_dim x1 -> x0, other arithmetic: 2.2 us -> none  [on_device(): return (input_grad[None], weight_grads)]
    unnamed x37 -> x44, local copies, waits for them, and re-layouts: 15.7 us -> 17.6 us
    concatenate x1 -> x0, other arithmetic: 1.92 us -> none  [on_device(): jnp.concatenate([gw, gwo], axis=0).reshape(count, 4 * width // count, width)]
    convert_element_type x5 -> x0, local copies, waits for them, and re-layouts: 1.8 us -> none  [scatter_sum(): lax.dynamic_index_in_dim(halves, 1 - bit, 1, keepdims=False).astype(BF16)]
    ppermute x5, waiting for transfers between devices: 21.6 us -> 19.8 us  [the longest x4 17.3 us: scatter_sum(): lax.ppermute(send, axes, [(d, d ^ steps[d & 1]) for d in range(count)])]
  transfers between devices with their start and end apart: 7 -> 7, of which waited for: 3 -> 4; matrix products, arithmetic and copies ran while one was open for 4% -> 0% of each run, Pallas kernels for 21% -> 22%
where the time goes in v2:
time: 94.7 us; the launch traced here: 93.9 us
  Pallas kernels  43.3 us (46%)
  waiting for transfers between devices  19.8 us (21%)
  local copies, waits for them, and re-layouts  17.6 us (19%)
  starting transfers between devices  12.4 us (13%)
    pallas_call x10, Pallas kernels, call(): pl.pallas_call(kernel, out_shape=outs, in_specs=specs or [VMEM] * len(arg...  43.3 us
    unnamed x44, local copies, waits for them, and re-layouts  17.6 us
    ppermute x4, waiting for transfers between devices, scatter_sum(): lax.ppermute(send, axes, [(d, d ^ steps[d & 1]) for d in range(count)])  17.3 us
    ppermute x4, starting transfers between devices, scatter_sum(): lax.ppermute(send, axes, [(d, d ^ steps[d & 1]) for d in range(count)])  6.11 us
    ppermute x1, starting transfers between devices, scatter_sum(): got = lax.ppermute(send, axes, [(d, d ^ 1) for d in range(count)])  2.54 us
    ppermute x1, waiting for transfers between devices, scatter_sum(): got = lax.ppermute(send, axes, [(d, d ^ 1) for d in range(count)])  2.5 us
    ppermute x1, starting transfers between devices, on_device(): x_prev = lax.ppermute(x, 'tm', [(s, s + 1) for s in range(tm - 1)])  2.46 us
  transfers between devices with their start and end apart: 7, of which 4 were waited for; matrix products, arithmetic and copies ran while one was open for 0% of the time, Pallas kernels for 22%

profile of v2, /device:TPU:0, one launch (start us, length us, event | category | flops | bytes accessed | tf_op | source)
XLA Modules:
  0.0 93.9 jit_solution(690902823784691801)
XLA Ops:
  0.6 2.5 %collective-permute-start = (bf16[1024,512]{1,0:T(8,128)(2,1)}, bf16[1024,512]{1,0:T(8,128)(2,1)S(1)}, u32[]{:S(2)}, u32[]{:S(2)}) collective-permute-start(bf16[1024,512]{1,0:T(8,128)(2,1)} %bitcast.11), channel_id=1, source_target_pairs={{0,1},{1,2},{2,3},{4,5},{5,6},{6,7},{8,9},{9,10},{10,11},{12,13},{... | collective-permute-start | bytes 3145736 | tf_op jit(solution)/shard_map/ppermute | solution.py:295
  3.1 1.2 %copy-done.14 = bf16[1,1024,512]{2,1,0:T(8,128)(2,1)S(1)} copy-done((bf16[1,1024,512]{2,1,0:T(8,128)(2,1)S(1)}, bf16[1,1024,512]{2,1,0:T(8,128)(2,1)}, u32[]{:S(2)}) %copy-start.14) | copy-done | bytes 1048600
  4.3 1.2 %copy-done.15 = bf16[1,1024,512]{2,1,0:T(8,128)(2,1)S(1)} copy-done((bf16[1,1024,512]{2,1,0:T(8,128)(2,1)S(1)}, bf16[1,1024,512]{2,1,0:T(8,128)(2,1)}, u32[]{:S(2)}) %copy-start.15) | copy-done | bytes 1048600
  5.6 1.2 %copy-done.16 = bf16[1,1024,512]{2,1,0:T(8,128)(2,1)S(1)} copy-done((bf16[1,1024,512]{2,1,0:T(8,128)(2,1)S(1)}, bf16[1,1024,512]{2,1,0:T(8,128)(2,1)}, u32[]{:S(2)}) %copy-start.16) | copy-done | bytes 1048600
  7.8 1.0 %copy-done.18 = bf16[512,512]{1,0:T(8,128)(2,1)S(1)} copy-done((bf16[512,512]{1,0:T(8,128)(2,1)S(1)}, bf16[512,512]{1,0:T(8,128)(2,1)}, u32[]{:S(2)}) %copy-start.18) | copy-done | bytes 524312
  8.9 1.0 %copy-done.19 = bf16[512,512]{1,0:T(8,128)(2,1)S(1)} copy-done((bf16[512,512]{1,0:T(8,128)(2,1)S(1)}, bf16[512,512]{1,0:T(8,128)(2,1)}, u32[]{:S(2)}) %copy-start.19) | copy-done | bytes 524312
  11.7 17.8 %shard_map.95 = (bf16[1024,512]{1,0:T(8,128)(2,1)S(1)}, bf16[1024,512]{1,0:T(8,128)(2,1)S(1)}, bf16[512,1024]{1,0:T(8,128)(2,1)S(1)}, bf16[512,1024]{1,0:T(8,128...) custom-call(bf16[1024,512]{1,0:T(8,128)(2,1)S(1)} %bitcast.12, ...), custom_call_target="tpu_custom_call" | custom-call | flops 5368709120 | bytes 5275648 | tf_op jit(solution)/shard_map/pallas_call | solution.py:246
  29.6 16.5 %shard_map.96 = (bf16[1024,512]{1,0:T(8,128)(2,1)S(1)}, bf16[512,1024]{1,0:T(8,128)(2,1)}, bf16[512,1024]{1,0:T(8,128)(2,1)S(1)}, bf16[512,1024]{1,0:T(8,128)(2,1)S(1)}, bf16[512,1024]{1,0:T(8,128)(2,1)S(1)}) custom-call(bf16[1024,512]{1,0:T(8,128)(2,1)S(1)} %collective-permute-done.xp_ref, bf16[512,512]{1,0:T(8,128)(2,1)S(1)} %get-tuple-element.30.wk_ref, ...), custom_call_target="tpu_custom_call" | custom-call | flops 5368709120 | bytes 8912896 | tf_op jit(solution)/shard_map/pallas_call | solution.py:246
  46.1 4.1 %shard_map.99 = (bf16[1024,512]{1,0:T(8,128)(2,1)}, f32[1024,512]{1,0:T(8,128)S(1)}) custom-call(bf16[512,1024]{1,0:T(8,128)(2,1)S(1)} %get-tuple-element.43.xt_ref, bf16[512,1024]{1,0:T(8,128)(2,1)S(1)} %get-tuple-element.44.xpt_ref, bf16[1024,512]{1,0:T(8,128)(2,1)S(1)} %get-tuple-element.38.dq_ref, bf16[512,1024]{1,0:T(8,128)(2,1)S(1)} %get-tuple-element.39.dkt_ref, ...), custom_call_target="tpu_custom_call" | custom-call | flops 2684354560 | bytes 8388608 | tf_op jit(solution)/shard_map/pallas_call | solution.py:246
  50.2 2.5 %collective-permute-start.2 = (bf16[1024,512]{1,0:T(8,128)(2,1)}, bf16[1024,512]{1,0:T(8,128)(2,1)S(1)}, u32[]{:S(2)}, u32[]{:S(2)}) collective-permute-start(bf16[1024,512]{1,0:T(8,128)(2,1)} %get-tuple-element.49), channel_id=1, source_target_pairs={{0,1},{1,0},{2,3},{3,2},{4,5},{5,4},{6,7},{7,6},{8,9},{9,8},{10,11... | collective-permute-start | bytes 3145736 | tf_op jit(solution)/shard_map/ppermute | solution.py:269
  52.7 2.5 %collective-permute-done.2.got_ref = bf16[1024,512]{1,0:T(8,128)(2,1)S(1)} collective-permute-done((bf16[1024,512]{1,0:T(8,128)(2,1)}, bf16[1024,512]{1,0:T(8,128)(2,1)S(1)}, u32[]{:S(2)}, u32[]{:S(2)}) %collective-permute-start.2) | collective-permute-done | bytes 1048608 | tf_op jit(solution)/shard_map/ppermute | solution.py:269
  57.4 1.3 %collective-permute-start.1 = (bf16[512,1024]{1,0:T(8,128)(2,1)}, bf16[512,1024]{1,0:T(8,128)(2,1)S(1)}, u32[]{:S(2)}, u32[]{:S(2)}) collective-permute-start(bf16[512,1024]{1,0:T(8,128)(2,1)} %get-tuple-element.42), channel_id=1, source_target_pairs={{1,0},{2,1},{3,2},{5,4},{6,5},{7,6},{9,8},{10,9},{11,10},{13,12},{... | collective-permute-start | bytes 3145736 | tf_op jit(solution)/shard_map/ppermute | solution.py:319
  58.7 7.8 %collective-permute-done.3.got_ref = bf16[512,512]{1,0:T(8,128)(2,1)S(1)} collective-permute-done((bf16[512,512]{1,0:T(8,128)(2,1)}, bf16[512,512]{1,0:T(8,128)(2,1)S(1)}, u32[]{:S(2)}, u32[]{:S(2)}) %collective-permute-start.3) | collective-permute-done | bytes 524320 | tf_op jit(solution)/shard_map/ppermute | solution.py:284
  66.5 1.2 %copy-done.1 = f32[512,512]{1,0:T(8,128)S(1)} copy-done((f32[512,512]{1,0:T(8,128)S(1)}, f32[512,512]{1,0:T(8,128)}, u32[]{:S(2)}) %copy-start.1) | copy-done | bytes 1048600
  67.9 1.6 %collective-permute-start.4 = (bf16[256,512]{1,0:T(8,128)(2,1)S(1)}, bf16[256,512]{1,0:T(8,128)(2,1)S(1)}, u32[]{:S(2)}, u32[]{:S(2)}) collective-permute-start(bf16[256,512]{1,0:T(8,128)(2,1)S(1)} %get-tuple-element.53), channel_id=1, source_target_pairs={{0,4},{1,3},{2,6},{3,1},{4,0},{5,7},{6,2},{7,5},{8,12},{9,11},{10,... | collective-permute-start | bytes 786440 | tf_op jit(solution)/shard_map/ppermute | solution.py:284
  69.4 4.9 %collective-permute-done.4.got_ref = bf16[256,512]{1,0:T(8,128)(2,1)S(1)} collective-permute-done((bf16[256,512]{1,0:T(8,128)(2,1)S(1)}, bf16[256,512]{1,0:T(8,128)(2,1)S(1)}, u32[]{:S(2)}, u32[]{:S(2)}) %collective-permute-start.4) | collective-permute-done | bytes 262176 | tf_op jit(solution)/shard_map/ppermute | solution.py:284
  74.3 1.6 %collective-permute-start.5 = (bf16[128,512]{1,0:T(8,128)(2,1)S(1)}, bf16[128,512]{1,0:T(8,128)(2,1)S(1)}, u32[]{:S(2)}, u32[]{:S(2)}) collective-permute-start(bf16[128,512]{1,0:T(8,128)(2,1)S(1)} %get-tuple-element.55), channel_id=1, source_target_pairs={{0,8},{1,9},{2,10},{3,11},{4,12},{5,13},{6,14},{7,15},{8,0},{9,1},... | collective-permute-start | bytes 393224 | tf_op jit(solution)/shard_map/ppermute | solution.py:284
  76.0 4.6 %collective-permute-done.5.got_ref = bf16[128,512]{1,0:T(8,128)(2,1)S(1)} collective-permute-done((bf16[128,512]{1,0:T(8,128)(2,1)S(1)}, bf16[128,512]{1,0:T(8,128)(2,1)S(1)}, u32[]{:S(2)}, u32[]{:S(2)}) %collective-permute-start.5) | collective-permute-done | bytes 131104 | tf_op jit(solution)/shard_map/ppermute | solution.py:284
  80.6 2.6 %collective-permute-start.6 = (bf16[64,512]{1,0:T(8,128)(2,1)S(1)}, bf16[64,512]{1,0:T(8,128)(2,1)S(1)}, u32[]{:S(2)}, u32[]{:S(2)}) collective-permute-start(bf16[64,512]{1,0:T(8,128)(2,1)S(1)} %get-tuple-element.57), channel_id=1, source_target_pairs={{0,16},{1,17},{2,18},{3,19},{4,20},{5,21},{6,22},{7,23},{8,24},{9,... | collective-permute-start | bytes 196616 | tf_op jit(solution)/shard_map/ppermute | solution.py:284
  83.2 1.2 %copy-done.3 = bf16[512,1024]{1,0:T(8,128)(2,1)S(1)} copy-done((bf16[512,1024]{1,0:T(8,128)(2,1)S(1)}, bf16[512,1024]{1,0:T(8,128)(2,1)}, u32[]{:S(2)}) %copy-start.3) | copy-done | bytes 1048600
  84.5 1.2 %copy-done.5 = bf16[512,1024]{1,0:T(8,128)(2,1)S(1)} copy-done((bf16[512,1024]{1,0:T(8,128)(2,1)S(1)}, bf16[512,1024]{1,0:T(8,128)(2,1)}, u32[]{:S(2)}) %copy-start.5) | copy-done | bytes 1048600
  85.7 1.2 %copy-done.7 = bf16[1024,512]{1,0:T(8,128)(2,1)S(1)} copy-done((bf16[1024,512]{1,0:T(8,128)(2,1)S(1)}, bf16[1024,512]{1,0:T(8,128)(2,1)}, u32[]{:S(2)}) %copy-start.7) | copy-done | bytes 1048600
  90.0 1.8 %shard_map.97.near_ref = f32[512,1024]{1,0:T(8,128)S(1)} custom-call(bf16[1024,512]{1,0:T(8,128)(2,1)S(1)} %copy-done.7, bf16[512,1024]{1,0:T(8,128)(2,1)S(1)} %copy-done.3, bf16[512,1024]{1,0:T(8,128)(2,1)S(1)} %copy-done.5, bf16[512,512]{1,0:T(8,128)(2,1)S(1)} %copy-done.9, bf16[512,512]{1,0:T(8,128)(2,1)S(1)} %copy-done.11, bf16[512,512]{1,0:T(8,128)(2,1)S(1)} %copy-done.13), custom_call_target="tpu_custom_call" | custom-call | flops 1610612736 | bytes 4718592 | tf_op jit(solution)/shard_map/pallas_call | solution.py:246
  91.8 1.3 %shard_map.98 = bf16[1024,512]{1,0:T(8,128)(2,1)} custom-call(f32[512,1024]{1,0:T(8,128)S(1)} %shard_map.97.near_ref, bf16[512,1024]{1,0:T(8,128)(2,1)S(1)} %collective-permute-done.1.back_ref), custom_call_target="tpu_custom_call" | custom-call | flops 67108864 | bytes 3145728 | tf_op jit(solution)/shard_map/pallas_call | solution.py:246
  (44 shorter events, 9.0 us)
Async XLA Ops:
  0.6 28.9 %collective-permute-start = (bf16[1024,512]{1,0:T(8,128)(2,1)}, bf16[1024,512]{1,0:T(8,128)(2,1)S(1)}, u32[]{:S(2)}, u32[]{:S(2)}) collective-permute-start(bf16[1024,512]{1,0:T(8,128)(2,1)} %bitcast.11), channel_id=1, source_target_pairs={{0,1},{1,2},{2,3},{4,5},{5,6},{6,7},{8,9},{9,10},{10,11},{12,13},{... | collective-permute-start | bytes 3145736 | tf_op jit(solution)/shard_map/ppermute | solution.py:295
  3.1 1.2 %copy-start.14 = (bf16[1,1024,512]{2,1,0:T(8,128)(2,1)S(1)}, bf16[1,1024,512]{2,1,0:T(8,128)(2,1)}, u32[]{:S(2)}) copy-start(bf16[1,1024,512]{2,1,0:T(8,128)(2,1)} %param.13) | copy-start | bytes 3145732
  4.3 1.2 %copy-start.15 = (bf16[1,1024,512]{2,1,0:T(8,128)(2,1)S(1)}, bf16[1,1024,512]{2,1,0:T(8,128)(2,1)}, u32[]{:S(2)}) copy-start(bf16[1,1024,512]{2,1,0:T(8,128)(2,1)} %param.15) | copy-start | bytes 3145732
  5.6 1.2 %copy-start.16 = (bf16[1,1024,512]{2,1,0:T(8,128)(2,1)S(1)}, bf16[1,1024,512]{2,1,0:T(8,128)(2,1)}, u32[]{:S(2)}) copy-start(bf16[1,1024,512]{2,1,0:T(8,128)(2,1)} %param.8) | copy-start | bytes 3145732
  7.8 1.0 %copy-start.18 = (bf16[512,512]{1,0:T(8,128)(2,1)S(1)}, bf16[512,512]{1,0:T(8,128)(2,1)}, u32[]{:S(2)}) copy-start(bf16[512,512]{1,0:T(8,128)(2,1)} %wk_hbm.1) | copy-start | bytes 1572868
  8.9 1.0 %copy-start.19 = (bf16[512,512]{1,0:T(8,128)(2,1)S(1)}, bf16[512,512]{1,0:T(8,128)(2,1)}, u32[]{:S(2)}) copy-start(bf16[512,512]{1,0:T(8,128)(2,1)} %wv_hbm.1) | copy-start | bytes 1572868
  9.9 1.0 %copy-start.20 = (bf16[512,512]{1,0:T(8,128)(2,1)S(1)}, bf16[512,512]{1,0:T(8,128)(2,1)}, u32[]{:S(2)}) copy-start(bf16[512,512]{1,0:T(8,128)(2,1)} %wo_hbm.1) | copy-start | bytes 1572868
  29.5 16.5 %copy-start.8 = (bf16[512,512]{1,0:T(8,128)(2,1)}, bf16[512,512]{1,0:T(8,128)(2,1)S(1)}, u32[]{:S(2)}) copy-start(bf16[512,512]{1,0:T(8,128)(2,1)S(1)} %get-tuple-element.41.wq_ref) | copy-start | bytes 1572868
  29.5 16.5 %copy-start.10 = (bf16[512,512]{1,0:T(8,128)(2,1)}, bf16[512,512]{1,0:T(8,128)(2,1)S(1)}, u32[]{:S(2)}) copy-start(bf16[512,512]{1,0:T(8,128)(2,1)S(1)} %get-tuple-element.30.wk_ref) | copy-start | bytes 1572868
  29.5 16.5 %copy-start.12 = (bf16[512,512]{1,0:T(8,128)(2,1)}, bf16[512,512]{1,0:T(8,128)(2,1)S(1)}, u32[]{:S(2)}) copy-start(bf16[512,512]{1,0:T(8,128)(2,1)S(1)} %get-tuple-element.31.wv_ref) | copy-start | bytes 1572868
  29.6 16.5 %copy-start.2 = (bf16[512,1024]{1,0:T(8,128)(2,1)}, bf16[512,1024]{1,0:T(8,128)(2,1)S(1)}, u32[]{:S(2)}) copy-start(bf16[512,1024]{1,0:T(8,128)(2,1)S(1)} %get-tuple-element.39.dkt_ref) | copy-start | bytes 3145732
  29.6 16.5 %copy-start.4 = (bf16[512,1024]{1,0:T(8,128)(2,1)}, bf16[512,1024]{1,0:T(8,128)(2,1)S(1)}, u32[]{:S(2)}) copy-start(bf16[512,1024]{1,0:T(8,128)(2,1)S(1)} %get-tuple-element.40.dvt_ref) | copy-start | bytes 3145732
  46.1 4.1 %copy-start.6 = (bf16[1024,512]{1,0:T(8,128)(2,1)}, bf16[1024,512]{1,0:T(8,128)(2,1)S(1)}, u32[]{:S(2)}) copy-start(bf16[1024,512]{1,0:T(8,128)(2,1)S(1)} %get-tuple-element.38.dq_ref) | copy-start | bytes 3145732
  50.2 5.0 %collective-permute-start.2 = (bf16[1024,512]{1,0:T(8,128)(2,1)}, bf16[1024,512]{1,0:T(8,128)(2,1)S(1)}, u32[]{:S(2)}, u32[]{:S(2)}) collective-permute-start(bf16[1024,512]{1,0:T(8,128)(2,1)} %get-tuple-element.49), channel_id=1, source_target_pairs={{0,1},{1,0},{2,3},{3,2},{4,5},{5,4},{6,7},{7,6},{8,9},{9,8},{10,11... | collective-permute-start | bytes 3145736 | tf_op jit(solution)/shard_map/ppermute | solution.py:269
  57.1 9.4 %collective-permute-start.3 = (bf16[512,512]{1,0:T(8,128)(2,1)}, bf16[512,512]{1,0:T(8,128)(2,1)S(1)}, u32[]{:S(2)}, u32[]{:S(2)}) collective-permute-start(bf16[512,512]{1,0:T(8,128)(2,1)} %get-tuple-element.51), channel_id=1, source_target_pairs={{0,2},{1,5},{2,0},{3,7},{4,6},{5,1},{6,4},{7,3},{8,10},{9,13},{10,... | collective-permute-start | bytes 1572872 | tf_op jit(solution)/shard_map/ppermute | solution.py:284
  57.4 34.4 %collective-permute-start.1 = (bf16[512,1024]{1,0:T(8,128)(2,1)}, bf16[512,1024]{1,0:T(8,128)(2,1)S(1)}, u32[]{:S(2)}, u32[]{:S(2)}) collective-permute-start(bf16[512,1024]{1,0:T(8,128)(2,1)} %get-tuple-element.42), channel_id=1, source_target_pairs={{1,0},{2,1},{3,2},{5,4},{6,5},{7,6},{9,8},{10,9},{11,10},{13,12},{... | collective-permute-start | bytes 3145736 | tf_op jit(solution)/shard_map/ppermute | solution.py:319
  66.5 1.2 %copy-start.1 = (f32[512,512]{1,0:T(8,128)S(1)}, f32[512,512]{1,0:T(8,128)}, u32[]{:S(2)}) copy-start(f32[512,512]{1,0:T(8,128)} %copy-done) | copy-start | bytes 3145732
  67.9 6.4 %collective-permute-start.4 = (bf16[256,512]{1,0:T(8,128)(2,1)S(1)}, bf16[256,512]{1,0:T(8,128)(2,1)S(1)}, u32[]{:S(2)}, u32[]{:S(2)}) collective-permute-start(bf16[256,512]{1,0:T(8,128)(2,1)S(1)} %get-tuple-element.53), channel_id=1, source_target_pairs={{0,4},{1,3},{2,6},{3,1},{4,0},{5,7},{6,2},{7,5},{8,12},{9,11},{10,... | collective-permute-start | bytes 786440 | tf_op jit(solution)/shard_map/ppermute | solution.py:284
  74.3 6.2 %collective-permute-start.5 = (bf16[128,512]{1,0:T(8,128)(2,1)S(1)}, bf16[128,512]{1,0:T(8,128)(2,1)S(1)}, u32[]{:S(2)}, u32[]{:S(2)}) collective-permute-start(bf16[128,512]{1,0:T(8,128)(2,1)S(1)} %get-tuple-element.55), channel_id=1, source_target_pairs={{0,8},{1,9},{2,10},{3,11},{4,12},{5,13},{6,14},{7,15},{8,0},{9,1},... | collective-permute-start | bytes 393224 | tf_op jit(solution)/shard_map/ppermute | solution.py:284
  80.6 12.6 %collective-permute-start.6 = (bf16[64,512]{1,0:T(8,128)(2,1)S(1)}, bf16[64,512]{1,0:T(8,128)(2,1)S(1)}, u32[]{:S(2)}, u32[]{:S(2)}) collective-permute-start(bf16[64,512]{1,0:T(8,128)(2,1)S(1)} %get-tuple-element.57), channel_id=1, source_target_pairs={{0,16},{1,17},{2,18},{3,19},{4,20},{5,21},{6,22},{7,23},{8,24},{9,... | collective-permute-start | bytes 196616 | tf_op jit(solution)/shard_map/ppermute | solution.py:284
  83.2 1.2 %copy-start.3 = (bf16[512,1024]{1,0:T(8,128)(2,1)S(1)}, bf16[512,1024]{1,0:T(8,128)(2,1)}, u32[]{:S(2)}) copy-start(bf16[512,1024]{1,0:T(8,128)(2,1)} %copy-done.2) | copy-start | bytes 3145732
  84.5 1.2 %copy-start.5 = (bf16[512,1024]{1,0:T(8,128)(2,1)S(1)}, bf16[512,1024]{1,0:T(8,128)(2,1)}, u32[]{:S(2)}) copy-start(bf16[512,1024]{1,0:T(8,128)(2,1)} %copy-done.4) | copy-start | bytes 3145732
  85.7 1.2 %copy-start.7 = (bf16[1024,512]{1,0:T(8,128)(2,1)S(1)}, bf16[1024,512]{1,0:T(8,128)(2,1)}, u32[]{:S(2)}) copy-start(bf16[1024,512]{1,0:T(8,128)(2,1)} %copy-done.6) | copy-start | bytes 3145732
  86.9 1.0 %copy-start.9 = (bf16[512,512]{1,0:T(8,128)(2,1)S(1)}, bf16[512,512]{1,0:T(8,128)(2,1)}, u32[]{:S(2)}) copy-start(bf16[512,512]{1,0:T(8,128)(2,1)} %copy-done.8) | copy-start | bytes 1572868
  (5 other events, 4.9 us)

commit v3 on v2

--- a/solution.py
+++ b/solution.py
@@ -7,6 +7,7 @@
 from jax.experimental import pallas as pl
 from jax.experimental.pallas import tpu as pltpu
 from jax.sharding import PartitionSpec as P
+
 
 HEADS = 8
 HEAD_DIM = 64
@@ -107,7 +108,7 @@
     copies = [pltpu.make_async_copy(a, b, sems.at[i]) for i, (a, b) in enumerate(zip(sources, targets))]
     for copy in copies:
         copy.start()
-    bins, width = x_ref.shape
+    bins, _ = x_ref.shape
     tiles = [slice(b * TILE, (b + 1) * TILE) for b in range(bins // TILE)]
     copies[0].wait()
     copies[1].wait()
@@ -160,7 +161,7 @@
     dq_ref, back_ref, dkf, dvf, xpt,
     k_ref, v_ref, *scratch,
 ):
-    bins, width = xp_ref.shape
+    bins, _ = xp_ref.shape
     for b in range(bins // TILE):
         bs = slice(b * TILE, (b + 1) * TILE)
         xp = xp_ref[bs, :]
@@ -216,9 +217,10 @@
                     send_ref[at * rows : (at + 1) * rows, :] = block.astype(BF16)
 
 
-def halve_kernel(bit_ref, keep_ref, got_ref, send_ref, out_ref):
+def halve_kernel(even_bit, odd_bit, keep_ref, got_ref, send_ref, out_ref):
     half = out_ref.shape[0]
-    bit = bit_ref[0]
+    me = lax.axis_index(("dp", "tm"))
+    bit = jnp.where(me % 2 == 1, me >> odd_bit, me >> even_bit) & 1
     mine = pl.ds(pl.multiple_of(bit * half, half), half)
     other = pl.ds(pl.multiple_of((1 - bit) * half, half), half)
     send_ref[...] = (keep_ref[other, :] + got_ref[other, :].astype(F32)).astype(BF16)
@@ -263,22 +265,17 @@
 def scatter_sum(send, keep, axes):
     count = lax.axis_size(axes)
     bits = count.bit_length() - 1
-    me = lax.axis_index(axes)
-    odd = me % 2 == 1
     width = keep.shape[1]
     got = lax.ppermute(send, axes, [(d, d ^ 1) for d in range(count)])
     for even_bit, odd_bit in zip(bit_order(bits, 0), bit_order(bits, 1)):
         half = keep.shape[0] // 2
-        bit = jnp.where(odd, me >> odd_bit, me >> even_bit) & 1
         send, keep = call(
-            halve_kernel,
+            functools.partial(halve_kernel, even_bit, odd_bit),
             [pltpu.VMEM((half, width), BF16), pltpu.VMEM((half, width), F32)],
             [],
             keep.size,
-            bit.reshape(1).astype(jnp.int32),
             on_chip(keep),
             on_chip(got),
-            specs=[pl.BlockSpec(memory_space=pltpu.SMEM), VMEM, VMEM],
         )
         steps = (1 << even_bit, 1 << odd_bit)
         got = lax.ppermute(send, axes, [(d, d ^ steps[d & 1]) for d in range(count)])
@@ -306,7 +303,7 @@
             (tall, BF16), (square, BF16), (tall, BF16), (tall, BF16), ((HEADS, bins), F32), (tall, BF16), (tall, BF16),
         )] + [pltpu.SemaphoreType.DMA((8,))] + attention_scratch(bins),
         band,
-        x, w_query, w_key, w_value, w_out, saved, up, lse,
+        *[pltpu.with_memory_space_constraint(a, pltpu.HBM) for a in (x, w_query, w_key, w_value, w_out, saved, up, lse)],
         specs=[pl.BlockSpec(memory_space=pltpu.HBM)] * 8,
     )
     dq, back, dkf, dvf, xpt = call(
@@ -333,6 +330,7 @@
 
 def solution(mesh):
     rows, copied = P("dp", "tm", None), P()
+
     return jax.shard_map(
         on_device,
         mesh=mesh,

time: 94.7 us -> 75.1 us (0.79)
  local copies, waits for them, and re-layouts: 17.6 us -> 0 us
  Pallas kernels: 43.3 us -> 41.5 us
    unnamed x44 -> x0, local copies, waits for them, and re-layouts: 17.6 us -> none
    pallas_call x10, Pallas kernels: 43.3 us -> 41.5 us  [call(): pl.pallas_call(kernel, out_shape=outs, in_specs=specs or [VMEM] * len(arg...]
  transfers between devices with their start and end apart: 7 -> 7, of which waited for: 4 -> 5; matrix products, arithmetic and copies ran while one was open for 0% -> 0% of each run, Pallas kernels for 22% -> 30%
where the time goes in v3:
time: 75.1 us; the launch traced here: 75 us
  Pallas kernels  41.5 us (55%)
  waiting for transfers between devices  20.2 us (27%)
  starting transfers between devices  12.5 us (17%)
    pallas_call x10, Pallas kernels, call(): pl.pallas_call(kernel, out_shape=outs, in_specs=specs or [VMEM] * len(arg...  41.5 us
    ppermute x4, waiting for transfers between devices, scatter_sum(): lax.ppermute(send, axes, [(d, d ^ steps[d & 1]) for d in range(count)])  17.9 us
    ppermute x4, starting transfers between devices, scatter_sum(): lax.ppermute(send, axes, [(d, d ^ steps[d & 1]) for d in range(count)])  6.2 us
    ppermute x1, starting transfers between devices, scatter_sum(): got = lax.ppermute(send, axes, [(d, d ^ 1) for d in range(count)])  2.6 us
    ppermute x1, starting transfers between devices, on_device(): x_prev = lax.ppermute(x, 'tm', [(s, s + 1) for s in range(tm - 1)])  2.46 us
    ppermute x1, waiting for transfers between devices, scatter_sum(): got = lax.ppermute(send, axes, [(d, d ^ 1) for d in range(count)])  2.29 us
  transfers between devices with their start and end apart: 7, of which 5 were waited for; matrix products, arithmetic and copies ran while one was open for 0% of the time, Pallas kernels for 30%

profile of v3, /device:TPU:0, one launch (start us, length us, event | category | flops | bytes accessed | tf_op | source)
XLA Modules:
  0.0 75.0 jit_solution(11082419610757837735)
XLA Ops:
  0.6 2.5 %collective-permute-start = (bf16[1024,512]{1,0:T(8,128)(2,1)}, bf16[1024,512]{1,0:T(8,128)(2,1)S(1)}, u32[]{:S(2)}, u32[]{:S(2)}) collective-permute-start(bf16[1024,512]{1,0:T(8,128)(2,1)} %bitcast.8), channel_id=1, source_target_pairs={{0,1},{1,2},{2,3},{4,5},{5,6},{6,7},{8,9},{9,10},{10,11},{12,13},{... | collective-permute-start | bytes 3145736 | tf_op jit(solution)/shard_map/ppermute | solution.py:292
  3.1 18.9 %shard_map.95 = (bf16[1024,512]{1,0:T(8,128)(2,1)S(1)}, bf16[1024,512]{1,0:T(8,128)(2,1)S(1)}, bf16[512,1024]{1,0:T(8,128)(2,1)S(1)}, bf16[512,1024]{1,0:T(8,128...) custom-call(bf16[1024,512]{1,0:T(8,128)(2,1)} %bitcast.9, ...), custom_call_target="tpu_custom_call" | custom-call | flops 5368709120 | bytes 5275648 | tf_op jit(solution)/shard_map/pallas_call | solution.py:248
  22.1 0.0 collective-permute-done.xp_ref
  22.1 15.3 %shard_map.96 = (bf16[1024,512]{1,0:T(8,128)(2,1)S(1)}, bf16[512,1024]{1,0:T(8,128)(2,1)S(1)}, bf16[512,1024]{1,0:T(8,128)(2,1)S(1)}, bf16[512,1024]{1,0:T(8,128)(2,1)S(1)}, bf16[512,1024]{1,0:T(8,128)(2,1)S(1)}) custom-call(bf16[1024,512]{1,0:T(8,128)(2,1)S(1)} %collective-permute-done.xp_ref, bf16[512,512]{1,0:T(8,128)(2,1)S(1)} %get-tuple-element.30.wk_ref, ...), custom_call_target="tpu_custom_call" | custom-call | flops 5368709120 | bytes 8912896 | tf_op jit(solution)/shard_map/pallas_call | solution.py:248
  37.4 3.1 %shard_map.99 = (bf16[1024,512]{1,0:T(8,128)(2,1)S(1)}, f32[1024,512]{1,0:T(8,128)S(1)}) custom-call(bf16[512,1024]{1,0:T(8,128)(2,1)S(1)} %get-tuple-element.43.xt_ref, bf16[512,1024]{1,0:T(8,128)(2,1)S(1)} %get-tuple-element.44.xpt_ref, bf16[1024,512]{1,0:T(8,128)(2,1)S(1)} %get-tuple-element.38.dq_ref, bf16[512,1024]{1,0:T(8,128)(2,1)S(1)} %get-tuple-element.39.dkt_ref, ...), custom_call_target="tpu_custom_call" | custom-call | flops 2684354560 | bytes 8388608 | tf_op jit(solution)/shard_map/pallas_call | solution.py:248
  40.5 2.6 %collective-permute-start.2 = (bf16[1024,512]{1,0:T(8,128)(2,1)S(1)}, bf16[1024,512]{1,0:T(8,128)(2,1)S(1)}, u32[]{:S(2)}, u32[]{:S(2)}) collective-permute-start(bf16[1024,512]{1,0:T(8,128)(2,1)S(1)} %get-tuple-element.49), channel_id=1, source_target_pairs={{0,1},{1,0},{2,3},{3,2},{4,5},{5,4},{6,7},{7,6},{8,9},{9,8},{10,11... | collective-permute-start | bytes 3145736 | tf_op jit(solution)/shard_map/ppermute | solution.py:269
  43.1 2.3 %collective-permute-done.2.got_ref = bf16[1024,512]{1,0:T(8,128)(2,1)S(1)} collective-permute-done((bf16[1024,512]{1,0:T(8,128)(2,1)S(1)}, bf16[1024,512]{1,0:T(8,128)(2,1)S(1)}, u32[]{:S(2)}, u32[]{:S(2)}) %collective-permute-start.2) | collective-permute-done | bytes 1048608 | tf_op jit(solution)/shard_map/ppermute | solution.py:269
  45.4 0.2 shard_map.100
  45.6 0.3 collective-permute-start.3
  45.9 1.3 %collective-permute-start.1 = (bf16[512,1024]{1,0:T(8,128)(2,1)S(1)}, bf16[512,1024]{1,0:T(8,128)(2,1)S(1)}, u32[]{:S(2)}, u32[]{:S(2)}) collective-permute-start(bf16[512,1024]{1,0:T(8,128)(2,1)S(1)} %get-tuple-element.42), channel_id=1, source_target_pairs={{1,0},{2,1},{3,2},{5,4},{6,5},{7,6},{9,8},{10,9},{11,10},{13,12},{... | collective-permute-start | bytes 3145736 | tf_op jit(solution)/shard_map/ppermute | solution.py:316
  47.2 7.6 %collective-permute-done.3.got_ref = bf16[512,512]{1,0:T(8,128)(2,1)S(1)} collective-permute-done((bf16[512,512]{1,0:T(8,128)(2,1)S(1)}, bf16[512,512]{1,0:T(8,128)(2,1)S(1)}, u32[]{:S(2)}, u32[]{:S(2)}) %collective-permute-start.3) | collective-permute-done | bytes 524320 | tf_op jit(solution)/shard_map/ppermute | solution.py:281
  54.8 0.1 shard_map.101
  54.9 1.6 %collective-permute-start.4 = (bf16[256,512]{1,0:T(8,128)(2,1)S(1)}, bf16[256,512]{1,0:T(8,128)(2,1)S(1)}, u32[]{:S(2)}, u32[]{:S(2)}) collective-permute-start(bf16[256,512]{1,0:T(8,128)(2,1)S(1)} %get-tuple-element.53), channel_id=1, source_target_pairs={{0,4},{1,3},{2,6},{3,1},{4,0},{5,7},{6,2},{7,5},{8,12},{9,11},{10,... | collective-permute-start | bytes 786440 | tf_op jit(solution)/shard_map/ppermute | solution.py:281
  56.5 4.8 %collective-permute-done.4.got_ref = bf16[256,512]{1,0:T(8,128)(2,1)S(1)} collective-permute-done((bf16[256,512]{1,0:T(8,128)(2,1)S(1)}, bf16[256,512]{1,0:T(8,128)(2,1)S(1)}, u32[]{:S(2)}, u32[]{:S(2)}) %collective-permute-start.4) | collective-permute-done | bytes 262176 | tf_op jit(solution)/shard_map/ppermute | solution.py:281
  61.4 1.6 %collective-permute-start.5 = (bf16[128,512]{1,0:T(8,128)(2,1)S(1)}, bf16[128,512]{1,0:T(8,128)(2,1)S(1)}, u32[]{:S(2)}, u32[]{:S(2)}) collective-permute-start(bf16[128,512]{1,0:T(8,128)(2,1)S(1)} %get-tuple-element.55), channel_id=1, source_target_pairs={{0,8},{1,9},{2,10},{3,11},{4,12},{5,13},{6,14},{7,15},{8,0},{9,1},... | collective-permute-start | bytes 393224 | tf_op jit(solution)/shard_map/ppermute | solution.py:281
  63.0 4.6 %collective-permute-done.5.got_ref = bf16[128,512]{1,0:T(8,128)(2,1)S(1)} collective-permute-done((bf16[128,512]{1,0:T(8,128)(2,1)S(1)}, bf16[128,512]{1,0:T(8,128)(2,1)S(1)}, u32[]{:S(2)}, u32[]{:S(2)}) %collective-permute-start.5) | collective-permute-done | bytes 131104 | tf_op jit(solution)/shard_map/ppermute | solution.py:281
  67.6 2.6 %collective-permute-start.6 = (bf16[64,512]{1,0:T(8,128)(2,1)S(1)}, bf16[64,512]{1,0:T(8,128)(2,1)S(1)}, u32[]{:S(2)}, u32[]{:S(2)}) collective-permute-start(bf16[64,512]{1,0:T(8,128)(2,1)S(1)} %get-tuple-element.57), channel_id=1, source_target_pairs={{0,16},{1,17},{2,18},{3,19},{4,20},{5,21},{6,22},{7,23},{8,24},{9,... | collective-permute-start | bytes 196616 | tf_op jit(solution)/shard_map/ppermute | solution.py:281
  70.3 1.8 %shard_map.97.near_ref = f32[512,1024]{1,0:T(8,128)S(1)} custom-call(bf16[1024,512]{1,0:T(8,128)(2,1)S(1)} %get-tuple-element.38.dq_ref, bf16[512,1024]{1,0:T(8,128)(2,1)S(1)} %get-tuple-element.39.dkt_ref, bf16[512,1024]{1,0:T(8,128)(2,1)S(1)} %get-tuple-element.40.dvt_ref, bf16[512,512]{1,0:T(8,128)(2,1)S(1)} %get-tuple-element.41.wq_ref, ...), custom_call_target="tpu_custom_call" | custom-call | flops 1610612736 | bytes 4718592 | tf_op jit(solution)/shard_map/pallas_call | solution.py:248
  72.1 0.0 collective-permute-done.1.back_ref
  72.1 1.3 %shard_map.98 = bf16[1024,512]{1,0:T(8,128)(2,1)} custom-call(f32[512,1024]{1,0:T(8,128)S(1)} %shard_map.97.near_ref, bf16[512,1024]{1,0:T(8,128)(2,1)S(1)} %collective-permute-done.1.back_ref), custom_call_target="tpu_custom_call" | custom-call | flops 67108864 | bytes 3145728 | tf_op jit(solution)/shard_map/pallas_call | solution.py:248
  73.4 0.9 %collective-permute-done.6.got_ref = bf16[64,512]{1,0:T(8,128)(2,1)S(1)} collective-permute-done((bf16[64,512]{1,0:T(8,128)(2,1)S(1)}, bf16[64,512]{1,0:T(8,128)(2,1)S(1)}, u32[]{:S(2)}, u32[]{:S(2)}) %collective-permute-start.6) | collective-permute-done | bytes 65568 | tf_op jit(solution)/shard_map/ppermute | solution.py:281
  74.3 0.7 shard_map.104
  (2 shorter events, 0.1 us)
Async XLA Ops:
  0.6 21.4 %collective-permute-start = (bf16[1024,512]{1,0:T(8,128)(2,1)}, bf16[1024,512]{1,0:T(8,128)(2,1)S(1)}, u32[]{:S(2)}, u32[]{:S(2)}) collective-permute-start(bf16[1024,512]{1,0:T(8,128)(2,1)} %bitcast.8), channel_id=1, source_target_pairs={{0,1},{1,2},{2,3},{4,5},{5,6},{6,7},{8,9},{9,10},{10,11},{12,13},{... | collective-permute-start | bytes 3145736 | tf_op jit(solution)/shard_map/ppermute | solution.py:292
  40.5 4.9 %collective-permute-start.2 = (bf16[1024,512]{1,0:T(8,128)(2,1)S(1)}, bf16[1024,512]{1,0:T(8,128)(2,1)S(1)}, u32[]{:S(2)}, u32[]{:S(2)}) collective-permute-start(bf16[1024,512]{1,0:T(8,128)(2,1)S(1)} %get-tuple-element.49), channel_id=1, source_target_pairs={{0,1},{1,0},{2,3},{3,2},{4,5},{5,4},{6,7},{7,6},{8,9},{9,8},{10,11... | collective-permute-start | bytes 3145736 | tf_op jit(solution)/shard_map/ppermute | solution.py:269
  45.6 9.2 %collective-permute-start.3 = (bf16[512,512]{1,0:T(8,128)(2,1)S(1)}, bf16[512,512]{1,0:T(8,128)(2,1)S(1)}, u32[]{:S(2)}, u32[]{:S(2)}) collective-permute-start(bf16[512,512]{1,0:T(8,128)(2,1)S(1)} %get-tuple-element.51), channel_id=1, source_target_pairs={{0,2},{1,5},{2,0},{3,7},{4,6},{5,1},{6,4},{7,3},{8,10},{9,13},{10,... | collective-permute-start | bytes 1572872 | tf_op jit(solution)/shard_map/ppermute | solution.py:281
  45.9 26.2 %collective-permute-start.1 = (bf16[512,1024]{1,0:T(8,128)(2,1)S(1)}, bf16[512,1024]{1,0:T(8,128)(2,1)S(1)}, u32[]{:S(2)}, u32[]{:S(2)}) collective-permute-start(bf16[512,1024]{1,0:T(8,128)(2,1)S(1)} %get-tuple-element.42), channel_id=1, source_target_pairs={{1,0},{2,1},{3,2},{5,4},{6,5},{7,6},{9,8},{10,9},{11,10},{13,12},{... | collective-permute-start | bytes 3145736 | tf_op jit(solution)/shard_map/ppermute | solution.py:316
  54.9 6.4 %collective-permute-start.4 = (bf16[256,512]{1,0:T(8,128)(2,1)S(1)}, bf16[256,512]{1,0:T(8,128)(2,1)S(1)}, u32[]{:S(2)}, u32[]{:S(2)}) collective-permute-start(bf16[256,512]{1,0:T(8,128)(2,1)S(1)} %get-tuple-element.53), channel_id=1, source_target_pairs={{0,4},{1,3},{2,6},{3,1},{4,0},{5,7},{6,2},{7,5},{8,12},{9,11},{10,... | collective-permute-start | bytes 786440 | tf_op jit(solution)/shard_map/ppermute | solution.py:281
  61.4 6.2 %collective-permute-start.5 = (bf16[128,512]{1,0:T(8,128)(2,1)S(1)}, bf16[128,512]{1,0:T(8,128)(2,1)S(1)}, u32[]{:S(2)}, u32[]{:S(2)}) collective-permute-start(bf16[128,512]{1,0:T(8,128)(2,1)S(1)} %get-tuple-element.55), channel_id=1, source_target_pairs={{0,8},{1,9},{2,10},{3,11},{4,12},{5,13},{6,14},{7,15},{8,0},{9,1},... | collective-permute-start | bytes 393224 | tf_op jit(solution)/shard_map/ppermute | solution.py:281
  67.6 6.6 %collective-permute-start.6 = (bf16[64,512]{1,0:T(8,128)(2,1)S(1)}, bf16[64,512]{1,0:T(8,128)(2,1)S(1)}, u32[]{:S(2)}, u32[]{:S(2)}) collective-permute-start(bf16[64,512]{1,0:T(8,128)(2,1)S(1)} %get-tuple-element.57), channel_id=1, source_target_pairs={{0,16},{1,17},{2,18},{3,19},{4,20},{5,21},{6,22},{7,23},{8,24},{9,... | collective-permute-start | bytes 196616 | tf_op jit(solution)/shard_map/ppermute | solution.py:281

commit v4 on v3

--- a/solution.py
+++ b/solution.py
@@ -158,7 +158,7 @@
 
 def far_kernel(
     xp_ref, wk_ref, wv_ref, q_ref, do_ref, qt_ref, dot_ref, aux_ref, dqn_ref,
-    dq_ref, back_ref, dkf, dvf, xpt,
+    dq_ref, dkf, dvf, xpt,
     k_ref, v_ref, *scratch,
 ):
     bins, _ = xp_ref.shape
@@ -181,14 +181,16 @@
     attention(
         False, (q_ref, do_ref, qt_ref, dot_ref, k_ref, v_ref, aux_ref), scratch, put_query, put_key, put_value
     )
-    back_ref[...] = (mm(wk_ref[...], dkf[...], 1, 0) + mm(wv_ref[...], dvf[...], 1, 0)).astype(BF16)
+
+
+def back_kernel(dkf_ref, dvf_ref, wk_ref, wv_ref, out_ref):
+    out_ref[...] = (mm(wk_ref[...], dkf_ref[...], 1, 0) + mm(wv_ref[...], dvf_ref[...], 1, 0)).astype(BF16)
 
 
 def bit_order(bits, parity):
     rest = list(range(1, bits))
-    if parity and len(rest) > 1:
-        rest[0], rest[1] = rest[1], rest[0]
-    return rest
+    turn = (2, 1, 0) if parity == 0 else (1, 2, 0)
+    return [rest[t] for t in turn] + rest[3:] if len(rest) >= 3 else rest
 
 
 def place(device, order):
@@ -306,14 +308,13 @@
         *[pltpu.with_memory_space_constraint(a, pltpu.HBM) for a in (x, w_query, w_key, w_value, w_out, saved, up, lse)],
         specs=[pl.BlockSpec(memory_space=pltpu.HBM)] * 8,
     )
-    dq, back, dkf, dvf, xpt = call(
+    dq, dkf, dvf, xpt = call(
         far_kernel,
-        [pltpu.VMEM(s, BF16) for s in (tall, wide, wide, wide, wide)],
+        [pltpu.VMEM(s, BF16) for s in (tall, wide, wide, wide)],
         [pltpu.VMEM(tall, BF16), pltpu.VMEM(tall, BF16)] + attention_scratch(bins),
         band,
         on_chip(x_prev), wk, wv, q, do, qt, dot, aux, dqn,
     )
-    back = lax.ppermute(back, "tm", [(s + 1, s) for s in range(tm - 1)])
     half = (2 * width, width)
     send, keep = call(
         functools.partial(weight_kernel, count),
@@ -322,6 +323,8 @@
         5 * one,
         xt, xpt, dq, dkt, dvt, dkf, dvf, gwo,
     )
+    (back,) = call(back_kernel, [pltpu.VMEM(wide, BF16)], [], 2 * one, dkf, dvf, wk, wv)
+    back = lax.ppermute(back, "tm", [(s + 1, s) for s in range(tm - 1)])
     weight_grads = scatter_sum(send, keep, axes)
     (near_grad,) = call(near_input_kernel, [pltpu.VMEM(wide, F32)], [], 3 * one, dq, dkt, dvt, wq, wk, wv)
     (input_grad,) = call(input_kernel, [jax.ShapeDtypeStruct(tall, BF16)], [], one // 8, near_grad, on_chip(back))

time: 75.1 us -> 73 us (0.972)
  waiting for transfers between devices: 20.2 us -> 18.1 us
    ppermute x4, waiting for transfers between devices: 17.9 us -> 15.8 us  [scatter_sum(): lax.ppermute(send, axes, [(d, d ^ steps[d & 1]) for d in range(count)])]
    pallas_call x10 -> x11, Pallas kernels: 41.5 us -> 41.5 us  [call(): pl.pallas_call(kernel, out_shape=outs, in_specs=specs or [VMEM] * len(arg...]
  transfers between devices with their start and end apart: 7 -> 7, of which waited for: 5 -> 4; matrix products, arithmetic and copies ran while one was open for 0% -> 0% of each run, Pallas kernels for 30% -> 32%
where the time goes in v4:
time: 73 us; the launch traced here: 72.9 us
  Pallas kernels  41.5 us (57%)
  waiting for transfers between devices  18.1 us (25%)
  starting transfers between devices  12.6 us (17%)
    pallas_call x11, Pallas kernels, call(): pl.pallas_call(kernel, out_shape=outs, in_specs=specs or [VMEM] * len(arg...  41.5 us
    ppermute x4, waiting for transfers between devices, scatter_sum(): lax.ppermute(send, axes, [(d, d ^ steps[d & 1]) for d in range(count)])  15.8 us
    ppermute x4, starting transfers between devices, scatter_sum(): lax.ppermute(send, axes, [(d, d ^ steps[d & 1]) for d in range(count)])  6.21 us
    ppermute x1, starting transfers between devices, scatter_sum(): got = lax.ppermute(send, axes, [(d, d ^ 1) for d in range(count)])  2.6 us
    ppermute x1, starting transfers between devices, on_device(): x_prev = lax.ppermute(x, 'tm', [(s, s + 1) for s in range(tm - 1)])  2.46 us
    ppermute x1, waiting for transfers between devices, scatter_sum(): got = lax.ppermute(send, axes, [(d, d ^ 1) for d in range(count)])  2.29 us
  transfers between devices with their start and end apart: 7, of which 4 were waited for; matrix products, arithmetic and copies ran while one was open for 0% of the time, Pallas kernels for 32%

profile of v4, /device:TPU:0, one launch (start us, length us, event | category | flops | bytes accessed | tf_op | source)
XLA Modules:
  0.0 72.9 jit_solution(6062627328104135474)
XLA Ops:
  0.6 2.5 %collective-permute-start = (bf16[1024,512]{1,0:T(8,128)(2,1)}, bf16[1024,512]{1,0:T(8,128)(2,1)S(1)}, u32[]{:S(2)}, u32[]{:S(2)}) collective-permute-start(bf16[1024,512]{1,0:T(8,128)(2,1)} %bitcast.8), channel_id=1, source_target_pairs={{0,1},{1,2},{2,3},{4,5},{5,6},{6,7},{8,9},{9,10},{10,11},{12,13},{... | collective-permute-start | bytes 3145736 | tf_op jit(solution)/shard_map/ppermute | solution.py:294
  3.1 18.9 %shard_map.95 = (bf16[1024,512]{1,0:T(8,128)(2,1)S(1)}, bf16[1024,512]{1,0:T(8,128)(2,1)S(1)}, bf16[512,1024]{1,0:T(8,128)(2,1)S(1)}, bf16[512,1024]{1,0:T(8,128...) custom-call(bf16[1024,512]{1,0:T(8,128)(2,1)} %bitcast.9, ...), custom_call_target="tpu_custom_call" | custom-call | flops 5368709120 | bytes 5275648 | tf_op jit(solution)/shard_map/pallas_call | solution.py:250
  22.1 0.0 collective-permute-done.xp_ref
  22.1 14.1 %shard_map.96 = (bf16[1024,512]{1,0:T(8,128)(2,1)S(1)}, bf16[512,1024]{1,0:T(8,128)(2,1)S(1)}, bf16[512,1024]{1,0:T(8,128)(2,1)S(1)}, bf16[512,1024]{1,0:T(8,128)(2,1)S(1)}) custom-call(bf16[1024,512]{1,0:T(8,128)(2,1)S(1)} %collective-permute-done.xp_ref, bf16[512,512]{1,0:T(8,128)(2,1)S(1)} %get-tuple-element.29.wk_ref, ...), custom_call_target="tpu_custom_call" | custom-call | flops 5368709120 | bytes 8912896 | tf_op jit(solution)/shard_map/pallas_call | solution.py:250
  36.1 3.1 %shard_map.100 = (bf16[1024,512]{1,0:T(8,128)(2,1)S(1)}, f32[1024,512]{1,0:T(8,128)S(1)}) custom-call(bf16[512,1024]{1,0:T(8,128)(2,1)S(1)} %get-tuple-element.43.xt_ref, bf16[512,1024]{1,0:T(8,128)(2,1)S(1)} %get-tuple-element.44.xpt_ref, bf16[1024,512]{1,0:T(8,128)(2,1)S(1)} %get-tuple-element.37.dq_ref, bf16[512,1024]{1,0:T(8,128)(2,1)S(1)} %get-tuple-element.38.dkt_ref, ...), custom_call_target="tpu_custom_call" | custom-call | flops 2684354560 | bytes 8388608 | tf_op jit(solution)/shard_map/pallas_call | solution.py:250
  39.3 2.6 %collective-permute-start.2 = (bf16[1024,512]{1,0:T(8,128)(2,1)S(1)}, bf16[1024,512]{1,0:T(8,128)(2,1)S(1)}, u32[]{:S(2)}, u32[]{:S(2)}) collective-permute-start(bf16[1024,512]{1,0:T(8,128)(2,1)S(1)} %get-tuple-element.47), channel_id=1, source_target_pairs={{0,1},{1,0},{2,3},{3,2},{4,5},{5,4},{6,7},{7,6},{8,9},{9,8},{10,11... | collective-permute-start | bytes 3145736 | tf_op jit(solution)/shard_map/ppermute | solution.py:271
  41.9 2.3 %collective-permute-done.2.got_ref = bf16[1024,512]{1,0:T(8,128)(2,1)S(1)} collective-permute-done((bf16[1024,512]{1,0:T(8,128)(2,1)S(1)}, bf16[1024,512]{1,0:T(8,128)(2,1)S(1)}, u32[]{:S(2)}, u32[]{:S(2)}) %collective-permute-start.2) | collective-permute-done | bytes 1048608 | tf_op jit(solution)/shard_map/ppermute | solution.py:271
  44.2 0.2 shard_map.101
  44.3 1.6 %collective-permute-start.3 = (bf16[512,512]{1,0:T(8,128)(2,1)S(1)}, bf16[512,512]{1,0:T(8,128)(2,1)S(1)}, u32[]{:S(2)}, u32[]{:S(2)}) collective-permute-start(bf16[512,512]{1,0:T(8,128)(2,1)S(1)} %get-tuple-element.49), channel_id=1, source_target_pairs={{0,8},{1,5},{2,10},{3,7},{4,12},{5,1},{6,14},{7,3},{8,0},{9,13},{1... | collective-permute-start | bytes 1572872 | tf_op jit(solution)/shard_map/ppermute | solution.py:283
  46.0 1.2 %shard_map.98 = bf16[512,1024]{1,0:T(8,128)(2,1)S(1)} custom-call(bf16[512,1024]{1,0:T(8,128)(2,1)S(1)} %get-tuple-element.41.dkf_ref, bf16[512,1024]{1,0:T(8,128)(2,1)S(1)} %get-tuple-element.42.dvf_ref, bf16[512,512]{1,0:T(8,128)(2,1)S(1)} %get-tuple-element.29.wk_ref, bf16[512,512]{1,0:T(8,128)(2,1)S(1)} %get-tuple-element.30.wv_ref), custom_call_target="tpu_custom_call" | custom-call | flops 1073741824 | bytes 3145728 | tf_op jit(solution)/shard_map/pallas_call | solution.py:250
  47.2 1.3 %collective-permute-start.1 = (bf16[512,1024]{1,0:T(8,128)(2,1)S(1)}, bf16[512,1024]{1,0:T(8,128)(2,1)S(1)}, u32[]{:S(2)}, u32[]{:S(2)}) collective-permute-start(bf16[512,1024]{1,0:T(8,128)(2,1)S(1)} %shard_map.98), channel_id=1, source_target_pairs={{1,0},{2,1},{3,2},{5,4},{6,5},{7,6},{9,8},{10,9},{11,10},{13,12},{... | collective-permute-start | bytes 3145736 | tf_op jit(solution)/shard_map/ppermute | solution.py:327
  48.5 5.1 %collective-permute-done.3.got_ref = bf16[512,512]{1,0:T(8,128)(2,1)S(1)} collective-permute-done((bf16[512,512]{1,0:T(8,128)(2,1)S(1)}, bf16[512,512]{1,0:T(8,128)(2,1)S(1)}, u32[]{:S(2)}, u32[]{:S(2)}) %collective-permute-start.3) | collective-permute-done | bytes 524320 | tf_op jit(solution)/shard_map/ppermute | solution.py:283
  53.6 0.1 shard_map.102
  53.7 1.6 %collective-permute-start.4 = (bf16[256,512]{1,0:T(8,128)(2,1)S(1)}, bf16[256,512]{1,0:T(8,128)(2,1)S(1)}, u32[]{:S(2)}, u32[]{:S(2)}) collective-permute-start(bf16[256,512]{1,0:T(8,128)(2,1)S(1)} %get-tuple-element.51), channel_id=1, source_target_pairs={{0,4},{1,9},{2,6},{3,11},{4,0},{5,13},{6,2},{7,15},{8,12},{9,1},{1... | collective-permute-start | bytes 786440 | tf_op jit(solution)/shard_map/ppermute | solution.py:283
  55.3 4.8 %collective-permute-done.4.got_ref = bf16[256,512]{1,0:T(8,128)(2,1)S(1)} collective-permute-done((bf16[256,512]{1,0:T(8,128)(2,1)S(1)}, bf16[256,512]{1,0:T(8,128)(2,1)S(1)}, u32[]{:S(2)}, u32[]{:S(2)}) %collective-permute-start.4) | collective-permute-done | bytes 262176 | tf_op jit(solution)/shard_map/ppermute | solution.py:283
  60.2 0.3 collective-permute-start.5
  60.5 5.9 %collective-permute-done.5.got_ref = bf16[128,512]{1,0:T(8,128)(2,1)S(1)} collective-permute-done((bf16[128,512]{1,0:T(8,128)(2,1)S(1)}, bf16[128,512]{1,0:T(8,128)(2,1)S(1)}, u32[]{:S(2)}, u32[]{:S(2)}) %collective-permute-start.5) | collective-permute-done | bytes 131104 | tf_op jit(solution)/shard_map/ppermute | solution.py:283
  66.4 2.6 %collective-permute-start.6 = (bf16[64,512]{1,0:T(8,128)(2,1)S(1)}, bf16[64,512]{1,0:T(8,128)(2,1)S(1)}, u32[]{:S(2)}, u32[]{:S(2)}) collective-permute-start(bf16[64,512]{1,0:T(8,128)(2,1)S(1)} %get-tuple-element.55), channel_id=1, source_target_pairs={{0,16},{1,17},{2,18},{3,19},{4,20},{5,21},{6,22},{7,23},{8,24},{9,... | collective-permute-start | bytes 196616 | tf_op jit(solution)/shard_map/ppermute | solution.py:283
  69.1 1.8 %shard_map.97.near_ref = f32[512,1024]{1,0:T(8,128)S(1)} custom-call(bf16[1024,512]{1,0:T(8,128)(2,1)S(1)} %get-tuple-element.37.dq_ref, bf16[512,1024]{1,0:T(8,128)(2,1)S(1)} %get-tuple-element.38.dkt_ref, bf16[512,1024]{1,0:T(8,128)(2,1)S(1)} %get-tuple-element.39.dvt_ref, bf16[512,512]{1,0:T(8,128)(2,1)S(1)} %get-tuple-element.40.wq_ref, ...), custom_call_target="tpu_custom_call" | custom-call | flops 1610612736 | bytes 4718592 | tf_op jit(solution)/shard_map/pallas_call | solution.py:250
  70.8 0.0 collective-permute-done.1.back_ref
  70.9 1.3 %shard_map.99 = bf16[1024,512]{1,0:T(8,128)(2,1)} custom-call(f32[512,1024]{1,0:T(8,128)S(1)} %shard_map.97.near_ref, bf16[512,1024]{1,0:T(8,128)(2,1)S(1)} %collective-permute-done.1.back_ref), custom_call_target="tpu_custom_call" | custom-call | flops 67108864 | bytes 3145728 | tf_op jit(solution)/shard_map/pallas_call | solution.py:250
  72.2 0.0 collective-permute-done.6.got_ref
  72.2 0.7 shard_map.105
  (2 shorter events, 0.1 us)
Async XLA Ops:
  0.6 21.4 %collective-permute-start = (bf16[1024,512]{1,0:T(8,128)(2,1)}, bf16[1024,512]{1,0:T(8,128)(2,1)S(1)}, u32[]{:S(2)}, u32[]{:S(2)}) collective-permute-start(bf16[1024,512]{1,0:T(8,128)(2,1)} %bitcast.8), channel_id=1, source_target_pairs={{0,1},{1,2},{2,3},{4,5},{5,6},{6,7},{8,9},{9,10},{10,11},{12,13},{... | collective-permute-start | bytes 3145736 | tf_op jit(solution)/shard_map/ppermute | solution.py:294
  39.3 4.9 %collective-permute-start.2 = (bf16[1024,512]{1,0:T(8,128)(2,1)S(1)}, bf16[1024,512]{1,0:T(8,128)(2,1)S(1)}, u32[]{:S(2)}, u32[]{:S(2)}) collective-permute-start(bf16[1024,512]{1,0:T(8,128)(2,1)S(1)} %get-tuple-element.47), channel_id=1, source_target_pairs={{0,1},{1,0},{2,3},{3,2},{4,5},{5,4},{6,7},{7,6},{8,9},{9,8},{10,11... | collective-permute-start | bytes 3145736 | tf_op jit(solution)/shard_map/ppermute | solution.py:271
  44.3 9.2 %collective-permute-start.3 = (bf16[512,512]{1,0:T(8,128)(2,1)S(1)}, bf16[512,512]{1,0:T(8,128)(2,1)S(1)}, u32[]{:S(2)}, u32[]{:S(2)}) collective-permute-start(bf16[512,512]{1,0:T(8,128)(2,1)S(1)} %get-tuple-element.49), channel_id=1, source_target_pairs={{0,8},{1,5},{2,10},{3,7},{4,12},{5,1},{6,14},{7,3},{8,0},{9,13},{1... | collective-permute-start | bytes 1572872 | tf_op jit(solution)/shard_map/ppermute | solution.py:283
  47.2 23.6 %collective-permute-start.1 = (bf16[512,1024]{1,0:T(8,128)(2,1)S(1)}, bf16[512,1024]{1,0:T(8,128)(2,1)S(1)}, u32[]{:S(2)}, u32[]{:S(2)}) collective-permute-start(bf16[512,1024]{1,0:T(8,128)(2,1)S(1)} %shard_map.98), channel_id=1, source_target_pairs={{1,0},{2,1},{3,2},{5,4},{6,5},{7,6},{9,8},{10,9},{11,10},{13,12},{... | collective-permute-start | bytes 3145736 | tf_op jit(solution)/shard_map/ppermute | solution.py:327
  53.7 6.4 %collective-permute-start.4 = (bf16[256,512]{1,0:T(8,128)(2,1)S(1)}, bf16[256,512]{1,0:T(8,128)(2,1)S(1)}, u32[]{:S(2)}, u32[]{:S(2)}) collective-permute-start(bf16[256,512]{1,0:T(8,128)(2,1)S(1)} %get-tuple-element.51), channel_id=1, source_target_pairs={{0,4},{1,9},{2,6},{3,11},{4,0},{5,13},{6,2},{7,15},{8,12},{9,1},{1... | collective-permute-start | bytes 786440 | tf_op jit(solution)/shard_map/ppermute | solution.py:283
  60.2 6.2 %collective-permute-start.5 = (bf16[128,512]{1,0:T(8,128)(2,1)S(1)}, bf16[128,512]{1,0:T(8,128)(2,1)S(1)}, u32[]{:S(2)}, u32[]{:S(2)}) collective-permute-start(bf16[128,512]{1,0:T(8,128)(2,1)S(1)} %get-tuple-element.53), channel_id=1, source_target_pairs={{0,2},{1,3},{2,0},{3,1},{4,6},{5,7},{6,4},{7,5},{8,10},{9,11},{10,... | collective-permute-start | bytes 393224 | tf_op jit(solution)/shard_map/ppermute | solution.py:283
  66.4 5.8 %collective-permute-start.6 = (bf16[64,512]{1,0:T(8,128)(2,1)S(1)}, bf16[64,512]{1,0:T(8,128)(2,1)S(1)}, u32[]{:S(2)}, u32[]{:S(2)}) collective-permute-start(bf16[64,512]{1,0:T(8,128)(2,1)S(1)} %get-tuple-element.55), channel_id=1, source_target_pairs={{0,16},{1,17},{2,18},{3,19},{4,20},{5,21},{6,22},{7,23},{8,24},{9,... | collective-permute-start | bytes 196616 | tf_op jit(solution)/shard_map/ppermute | solution.py:283

commit v5 on v4

--- a/solution.py
+++ b/solution.py
@@ -34,8 +34,8 @@
 
 
 def attention(near, refs, scratch, put_query, put_key, put_value):
-    q_ref, do_ref, qt_ref, dot_ref, k_ref, v_ref, aux_ref = refs
-    km, vm, lseb, offb, prob, grad, acc = scratch
+    q_ref, do_ref, qt_ref, dot_ref, k_ref, v_ref, kt_ref, aux_ref = refs
+    km, vm, lseb, offb, prob, grad, grad_t = scratch
     bins = q_ref.shape[0]
     blocks = bins // TILE
 
@@ -67,7 +67,9 @@
                         p = jnp.where(r >= c if near else r < c, p, 0.0)
                     dp = mm(do_ref[qs, cols], vw, 1, 1)
                     prob[h, qs, ks] = p.astype(BF16)
-                    grad[h, qs, ks] = (p * (dp - twice(offb[qs, :]))).astype(BF16)
+                    g = (p * (dp - twice(offb[qs, :]))).astype(BF16)
+                    grad[h, qs, ks] = g
+                    grad_t[h, ks, qs] = g.T
             for j in range(blocks):
                 ks = slice(j * TILE, (j + 1) * TILE)
                 qs = slice(j * TILE, bins) if near else slice(0, (j + 1) * TILE)
@@ -76,11 +78,7 @@
             for i in range(blocks):
                 qs = slice(i * TILE, (i + 1) * TILE)
                 ks = slice(0, (i + 1) * TILE) if near else slice(i * TILE, bins)
-                part = mm(grad[h, qs, ks], km[h, ks, :], 1, 0)
-                if h == 0:
-                    acc[qs, :] = part
-                else:
-                    put_query(qs, cols, (acc[qs, :] + part) * SCALE)
+                put_query(rows, qs, mm(kt_ref[rows, ks], grad_t[h, ks, qs], 1, 0) * SCALE)
         return carry
 
     lax.fori_loop(0, HEADS // 2, body, 0)
@@ -94,14 +92,14 @@
         pltpu.VMEM((bins, 128), F32),
         pltpu.VMEM((2, bins, bins), BF16),
         pltpu.VMEM((2, bins, bins), BF16),
-        pltpu.VMEM((bins, 128), F32),
+        pltpu.VMEM((2, bins, bins), BF16),
     ]
 
 
 def near_kernel(
     x_hbm, wq_hbm, wk_hbm, wv_hbm, wo_hbm, saved_hbm, up_hbm, lse_hbm,
-    q_ref, do_ref, qt_ref, dot_ref, aux_ref, dq_ref, dkt_ref, dvt_ref, gwo_ref, xt_ref, wq_ref, wk_ref, wv_ref,
-    x_ref, wo_ref, saved_ref, up_ref, lse_ref, k_ref, v_ref, sems, *scratch,
+    q_ref, do_ref, qt_ref, dot_ref, aux_ref, dqt_ref, dkt_ref, dvt_ref, gwo_ref, xt_ref, wq_ref, wk_ref, wv_ref,
+    x_ref, wo_ref, saved_ref, up_ref, lse_ref, k_ref, v_ref, kt_ref, sems, *scratch,
 ):
     sources = (up_hbm, wo_hbm, x_hbm, wq_hbm, wk_hbm, wv_hbm, saved_hbm, lse_hbm)
     targets = (up_ref, wo_ref, x_ref, wq_ref, wk_ref, wv_ref, saved_ref, lse_ref)
@@ -126,7 +124,9 @@
     copies[4].wait()
     copies[5].wait()
     for bs in tiles:
-        k_ref[bs, :] = mm(x_ref[bs, :], wk_ref[...], 1, 0).astype(BF16)
+        k = mm(x_ref[bs, :], wk_ref[...], 1, 0).astype(BF16)
+        k_ref[bs, :] = k
+        kt_ref[:, bs] = k.T
         v_ref[bs, :] = mm(x_ref[bs, :], wv_ref[...], 1, 0).astype(BF16)
     copies[6].wait()
     copies[7].wait()
@@ -142,8 +142,8 @@
         aux_ref[bs, :] = aux
     gwo_ref[...] = mm(saved_ref[...], up_ref[...], 0, 0)
 
-    def put_query(qs, cols, value):
-        dq_ref[qs, cols] = value
+    def put_query(rows, qs, value):
+        dqt_ref[rows, qs] = value
 
     def put_key(rows, ks, value):
         dkt_ref[rows, ks] = value.astype(BF16)
@@ -152,25 +152,27 @@
         dvt_ref[rows, ks] = value.astype(BF16)
 
     attention(
-        True, (q_ref, do_ref, qt_ref, dot_ref, k_ref, v_ref, aux_ref), scratch, put_query, put_key, put_value
+        True, (q_ref, do_ref, qt_ref, dot_ref, k_ref, v_ref, kt_ref, aux_ref), scratch, put_query, put_key, put_value
     )
 
 
 def far_kernel(
     xp_ref, wk_ref, wv_ref, q_ref, do_ref, qt_ref, dot_ref, aux_ref, dqn_ref,
-    dq_ref, dkf, dvf, xpt,
-    k_ref, v_ref, *scratch,
+    dqt_ref, dkf, dvf, xpt,
+    k_ref, v_ref, kt_ref, *scratch,
 ):
     bins, _ = xp_ref.shape
     for b in range(bins // TILE):
         bs = slice(b * TILE, (b + 1) * TILE)
         xp = xp_ref[bs, :]
-        k_ref[bs, :] = mm(xp, wk_ref[...], 1, 0).astype(BF16)
+        k = mm(xp, wk_ref[...], 1, 0).astype(BF16)
+        k_ref[bs, :] = k
+        kt_ref[:, bs] = k.T
         v_ref[bs, :] = mm(xp, wv_ref[...], 1, 0).astype(BF16)
         xpt[:, bs] = xp.T
 
-    def put_query(qs, cols, value):
-        dq_ref[qs, cols] = (dqn_ref[qs, cols] + value).astype(BF16)
+    def put_query(rows, qs, value):
+        dqt_ref[rows, qs] = (dqn_ref[rows, qs] + value).astype(BF16)
 
     def put_key(rows, ks, value):
         dkf[rows, ks] = value.astype(BF16)
@@ -179,7 +181,7 @@
         dvf[rows, ks] = value.astype(BF16)
 
     attention(
-        False, (q_ref, do_ref, qt_ref, dot_ref, k_ref, v_ref, aux_ref), scratch, put_query, put_key, put_value
+        False, (q_ref, do_ref, qt_ref, dot_ref, k_ref, v_ref, kt_ref, aux_ref), scratch, put_query, put_key, put_value
     )
 
 
@@ -197,26 +199,22 @@
     return sum(((device >> bit) & 1) << (len(order) - 1 - t) for t, bit in enumerate(order))
 
 
-def weight_kernel(count, xt_ref, xpt_ref, dq_ref, dkt_ref, dvt_ref, dkf_ref, dvf_ref, gwo_ref, send_ref, keep_ref, sums):
+def weight_kernel(count, xt_ref, xpt_ref, dqt_ref, dkt_ref, dvt_ref, dkf_ref, dvf_ref, gwo_ref, send_ref, both_ref):
     width = xt_ref.shape[0]
-    sums[0:width, :] = mm(xt_ref[...], dq_ref[...], 1, 0)
-    sums[width : 2 * width, :] = mm(xt_ref[...], dkt_ref[...], 1, 1) + mm(xpt_ref[...], dkf_ref[...], 1, 1)
-    sums[2 * width : 3 * width, :] = mm(xt_ref[...], dvt_ref[...], 1, 1) + mm(xpt_ref[...], dvf_ref[...], 1, 1)
-    sums[3 * width :, :] = gwo_ref[...]
     rows = 4 * width // count
     bits = count.bit_length() - 1
-    mine = lax.axis_index("tm") % 2
-    for parity in range(2):
-
-        @pl.when(mine == parity)
-        def _(parity=parity):
-            for device in range(count):
-                at = place(device, bit_order(bits, device & 1))
-                block = sums[device * rows : (device + 1) * rows, :]
-                if device & 1 == parity:
-                    keep_ref[at * rows : (at + 1) * rows, :] = block
-                else:
-                    send_ref[at * rows : (at + 1) * rows, :] = block.astype(BF16)
+
+    def put(which, value):
+        for block in range(width // rows):
+            device = which * (width // rows) + block
+            at = place(device, bit_order(bits, device & 1))
+            both_ref[device & 1, at * rows : (at + 1) * rows, :] = value[block * rows : (block + 1) * rows, :]
+
+    put(0, mm(xt_ref[...], dqt_ref[...], 1, 1))
+    put(1, mm(xt_ref[...], dkt_ref[...], 1, 1) + mm(xpt_ref[...], dkf_ref[...], 1, 1))
+    put(2, mm(xt_ref[...], dvt_ref[...], 1, 1) + mm(xpt_ref[...], dvf_ref[...], 1, 1))
+    put(3, gwo_ref[...])
+    send_ref[...] = both_ref[1 - lax.axis_index(("dp", "tm")) % 2].astype(BF16)
 
 
 def halve_kernel(even_bit, odd_bit, keep_ref, got_ref, send_ref, out_ref):
@@ -225,8 +223,9 @@
     bit = jnp.where(me % 2 == 1, me >> odd_bit, me >> even_bit) & 1
     mine = pl.ds(pl.multiple_of(bit * half, half), half)
     other = pl.ds(pl.multiple_of((1 - bit) * half, half), half)
-    send_ref[...] = (keep_ref[other, :] + got_ref[other, :].astype(F32)).astype(BF16)
-    out_ref[...] = keep_ref[mine, :] + got_ref[mine, :].astype(F32)
+    kept = keep_ref.at[me % 2] if len(keep_ref.shape) == 3 else keep_ref
+    send_ref[...] = (kept[other, :] + got_ref[other, :].astype(F32)).astype(BF16)
+    out_ref[...] = kept[mine, :] + got_ref[mine, :].astype(F32)
 
 
 def add_kernel(keep_ref, got_ref, out_ref):
@@ -235,7 +234,7 @@
 
 def near_input_kernel(dq_ref, dkt_ref, dvt_ref, wq_ref, wk_ref, wv_ref, out_ref):
     out_ref[...] = (
-        mm(wq_ref[...], dq_ref[...], 1, 1) + mm(wk_ref[...], dkt_ref[...], 1, 0) + mm(wv_ref[...], dvt_ref[...], 1, 0)
+        mm(wq_ref[...], dq_ref[...], 1, 0) + mm(wk_ref[...], dkt_ref[...], 1, 0) + mm(wv_ref[...], dvt_ref[...], 1, 0)
     )
 
 
@@ -246,7 +245,7 @@
         out_ref[bs, :] = (near_ref[:, bs] + back_ref[:, bs].astype(F32)).T.astype(BF16)
 
 
-def call(kernel, outs, scratch, flops, *args, specs=None, limit=24):
+def call(kernel, outs, scratch, flops, *args, specs=None, limit=28):
     return pl.pallas_call(
         kernel,
         out_shape=outs,
@@ -267,10 +266,10 @@
 def scatter_sum(send, keep, axes):
     count = lax.axis_size(axes)
     bits = count.bit_length() - 1
-    width = keep.shape[1]
+    width = keep.shape[-1]
     got = lax.ppermute(send, axes, [(d, d ^ 1) for d in range(count)])
     for even_bit, odd_bit in zip(bit_order(bits, 0), bit_order(bits, 1)):
-        half = keep.shape[0] // 2
+        half = keep.shape[-2] // 2
         send, keep = call(
             functools.partial(halve_kernel, even_bit, odd_bit),
             [pltpu.VMEM((half, width), BF16), pltpu.VMEM((half, width), F32)],
@@ -298,11 +297,11 @@
     q, do, qt, dot, aux, dqn, dkt, dvt, gwo, xt, wq, wk, wv = call(
         near_kernel,
         [pltpu.VMEM(s, d) for s, d in (
-            (tall, BF16), (tall, BF16), (wide, BF16), (wide, BF16), ((bins, 128), F32), (tall, F32), (wide, BF16),
+            (tall, BF16), (tall, BF16), (wide, BF16), (wide, BF16), ((bins, 128), F32), (wide, F32), (wide, BF16),
             (wide, BF16), (square, F32), (wide, BF16), (square, BF16), (square, BF16), (square, BF16),
         )],
         [pltpu.VMEM(s, d) for s, d in (
-            (tall, BF16), (square, BF16), (tall, BF16), (tall, BF16), ((HEADS, bins), F32), (tall, BF16), (tall, BF16),
+            (tall, BF16), (square, BF16), (tall, BF16), (tall, BF16), ((HEADS, bins), F32), (tall, BF16), (tall, BF16), (wide, BF16),
         )] + [pltpu.SemaphoreType.DMA((8,))] + attention_scratch(bins),
         band,
         *[pltpu.with_memory_space_constraint(a, pltpu.HBM) for a in (x, w_query, w_key, w_value, w_out, saved, up, lse)],
@@ -310,16 +309,16 @@
     )
     dq, dkf, dvf, xpt = call(
         far_kernel,
-        [pltpu.VMEM(s, BF16) for s in (tall, wide, wide, wide)],
-        [pltpu.VMEM(tall, BF16), pltpu.VMEM(tall, BF16)] + attention_scratch(bins),
+        [pltpu.VMEM(wide, BF16)] * 4,
+        [pltpu.VMEM(s, BF16) for s in (tall, tall, wide)] + attention_scratch(bins),
         band,
         on_chip(x_prev), wk, wv, q, do, qt, dot, aux, dqn,
     )
     half = (2 * width, width)
     send, keep = call(
         functools.partial(weight_kernel, count),
-        [pltpu.VMEM(half, BF16), pltpu.VMEM(half, F32)],
-        [pltpu.VMEM((4 * width, width), F32)],
+        [pltpu.VMEM(half, BF16), pltpu.VMEM((2, *half), F32)],
+        [],
         5 * one,
         xt, xpt, dq, dkt, dvt, dkf, dvf, gwo,
     )

time: 73 us -> 71.8 us (0.984)
  Pallas kernels: 41.5 us -> 40.3 us
    pallas_call x11, Pallas kernels: 41.5 us -> 40.3 us  [call(): pl.pallas_call(kernel, out_shape=outs, in_specs=specs or [VMEM] * len(arg...]
where the time goes in v5:
time: 71.8 us; the launch traced here: 71.6 us
  Pallas kernels  40.3 us (56%)
  waiting for transfers between devices  18.1 us (25%)
  starting transfers between devices  12.6 us (18%)
    pallas_call x11, Pallas kernels, call(): pl.pallas_call(kernel, out_shape=outs, in_specs=specs or [VMEM] * len(arg...  40.3 us
    ppermute x4, waiting for transfers between devices, scatter_sum(): lax.ppermute(send, axes, [(d, d ^ steps[d & 1]) for d in range(count)])  15.8 us
    ppermute x4, starting transfers between devices, scatter_sum(): lax.ppermute(send, axes, [(d, d ^ steps[d & 1]) for d in range(count)])  6.22 us
    ppermute x1, starting transfers between devices, scatter_sum(): got = lax.ppermute(send, axes, [(d, d ^ 1) for d in range(count)])  2.59 us
    ppermute x1, starting transfers between devices, on_device(): x_prev = lax.ppermute(x, 'tm', [(s, s + 1) for s in range(tm - 1)])  2.46 us
    ppermute x1, waiting for transfers between devices, scatter_sum(): got = lax.ppermute(send, axes, [(d, d ^ 1) for d in range(count)])  2.29 us
  transfers between devices with their start and end apart: 7, of which 4 were waited for; matrix products, arithmetic and copies ran while one was open for 0% of the time, Pallas kernels for 32%

profile of v5, /device:TPU:0, one launch (start us, length us, event | category | flops | bytes accessed | tf_op | source)
XLA Modules:
  0.0 71.6 jit_solution(2025290638099091850)
XLA Ops:
  0.6 2.5 %collective-permute-start = (bf16[1024,512]{1,0:T(8,128)(2,1)}, bf16[1024,512]{1,0:T(8,128)(2,1)S(1)}, u32[]{:S(2)}, u32[]{:S(2)}) collective-permute-start(bf16[1024,512]{1,0:T(8,128)(2,1)} %bitcast.8), channel_id=1, source_target_pairs={{0,1},{1,2},{2,3},{4,5},{5,6},{6,7},{8,9},{9,10},{10,11},{12,13},{... | collective-permute-start | bytes 3145736 | tf_op jit(solution)/shard_map/ppermute | solution.py:293
  3.1 18.3 %shard_map.95 = (bf16[1024,512]{1,0:T(8,128)(2,1)S(1)}, bf16[1024,512]{1,0:T(8,128)(2,1)S(1)}, bf16[512,1024]{1,0:T(8,128)(2,1)S(1)}, bf16[512,1024]{1,0:T(8,128...) custom-call(bf16[1024,512]{1,0:T(8,128)(2,1)} %bitcast.9, ...), custom_call_target="tpu_custom_call" | custom-call | flops 5368709120 | bytes 5275648 | tf_op jit(solution)/shard_map/pallas_call | solution.py:249
  21.4 0.0 collective-permute-done.xp_ref
  21.4 13.3 %shard_map.96 = (bf16[512,1024]{1,0:T(8,128)(2,1)S(1)}, bf16[512,1024]{1,0:T(8,128)(2,1)S(1)}, bf16[512,1024]{1,0:T(8,128)(2,1)S(1)}, bf16[512,1024]{1,0:T(8,128)(2,1)S(1)}) custom-call(bf16[1024,512]{1,0:T(8,128)(2,1)S(1)} %collective-permute-done.xp_ref, bf16[512,512]{1,0:T(8,128)(2,1)S(1)} %get-tuple-element.29.wk_ref, ...), custom_call_target="tpu_custom_call" | custom-call | flops 5368709120 | bytes 8912896 | tf_op jit(solution)/shard_map/pallas_call | solution.py:249
  34.7 3.3 %shard_map.100 = (bf16[1024,512]{1,0:T(8,128)(2,1)S(1)}, f32[2,1024,512]{2,1,0:T(8,128)S(1)}) custom-call(bf16[512,1024]{1,0:T(8,128)(2,1)S(1)} %get-tuple-element.43.xt_ref, bf16[512,1024]{1,0:T(8,128)(2,1)S(1)} %get-tuple-element.44.xpt_ref, bf16[512,1024]{1,0:T(8,128)(2,1)S(1)} %get-tuple-element.37.dq_ref.dqt_ref, ...), custom_call_target="tpu_custom_call" | custom-call | flops 2684354560 | bytes 8388608 | tf_op jit(solution)/shard_map/pallas_call | solution.py:249
  38.1 2.6 %collective-permute-start.2 = (bf16[1024,512]{1,0:T(8,128)(2,1)S(1)}, bf16[1024,512]{1,0:T(8,128)(2,1)S(1)}, u32[]{:S(2)}, u32[]{:S(2)}) collective-permute-start(bf16[1024,512]{1,0:T(8,128)(2,1)S(1)} %get-tuple-element.47), channel_id=1, source_target_pairs={{0,1},{1,0},{2,3},{3,2},{4,5},{5,4},{6,7},{7,6},{8,9},{9,8},{10,11... | collective-permute-start | bytes 3145736 | tf_op jit(solution)/shard_map/ppermute | solution.py:270
  40.6 2.3 %collective-permute-done.2.got_ref = bf16[1024,512]{1,0:T(8,128)(2,1)S(1)} collective-permute-done((bf16[1024,512]{1,0:T(8,128)(2,1)S(1)}, bf16[1024,512]{1,0:T(8,128)(2,1)S(1)}, u32[]{:S(2)}, u32[]{:S(2)}) %collective-permute-start.2) | collective-permute-done | bytes 1048608 | tf_op jit(solution)/shard_map/ppermute | solution.py:270
  42.9 0.2 shard_map.101
  43.1 1.6 %collective-permute-start.3 = (bf16[512,512]{1,0:T(8,128)(2,1)S(1)}, bf16[512,512]{1,0:T(8,128)(2,1)S(1)}, u32[]{:S(2)}, u32[]{:S(2)}) collective-permute-start(bf16[512,512]{1,0:T(8,128)(2,1)S(1)} %get-tuple-element.49), channel_id=1, source_target_pairs={{0,8},{1,5},{2,10},{3,7},{4,12},{5,1},{6,14},{7,3},{8,0},{9,13},{1... | collective-permute-start | bytes 1572872 | tf_op jit(solution)/shard_map/ppermute | solution.py:282
  44.7 1.2 %shard_map.98 = bf16[512,1024]{1,0:T(8,128)(2,1)S(1)} custom-call(bf16[512,1024]{1,0:T(8,128)(2,1)S(1)} %get-tuple-element.41.dkf_ref, bf16[512,1024]{1,0:T(8,128)(2,1)S(1)} %get-tuple-element.42.dvf_ref, bf16[512,512]{1,0:T(8,128)(2,1)S(1)} %get-tuple-element.29.wk_ref, bf16[512,512]{1,0:T(8,128)(2,1)S(1)} %get-tuple-element.30.wv_ref), custom_call_target="tpu_custom_call" | custom-call | flops 1073741824 | bytes 3145728 | tf_op jit(solution)/shard_map/pallas_call | solution.py:249
  46.0 1.3 %collective-permute-start.1 = (bf16[512,1024]{1,0:T(8,128)(2,1)S(1)}, bf16[512,1024]{1,0:T(8,128)(2,1)S(1)}, u32[]{:S(2)}, u32[]{:S(2)}) collective-permute-start(bf16[512,1024]{1,0:T(8,128)(2,1)S(1)} %shard_map.98), channel_id=1, source_target_pairs={{1,0},{2,1},{3,2},{5,4},{6,5},{7,6},{9,8},{10,9},{11,10},{13,12},{... | collective-permute-start | bytes 3145736 | tf_op jit(solution)/shard_map/ppermute | solution.py:326
  47.3 5.0 %collective-permute-done.3.got_ref = bf16[512,512]{1,0:T(8,128)(2,1)S(1)} collective-permute-done((bf16[512,512]{1,0:T(8,128)(2,1)S(1)}, bf16[512,512]{1,0:T(8,128)(2,1)S(1)}, u32[]{:S(2)}, u32[]{:S(2)}) %collective-permute-start.3) | collective-permute-done | bytes 524320 | tf_op jit(solution)/shard_map/ppermute | solution.py:282
  52.4 0.1 shard_map.102
  52.4 1.6 %collective-permute-start.4 = (bf16[256,512]{1,0:T(8,128)(2,1)S(1)}, bf16[256,512]{1,0:T(8,128)(2,1)S(1)}, u32[]{:S(2)}, u32[]{:S(2)}) collective-permute-start(bf16[256,512]{1,0:T(8,128)(2,1)S(1)} %get-tuple-element.51), channel_id=1, source_target_pairs={{0,4},{1,9},{2,6},{3,11},{4,0},{5,13},{6,2},{7,15},{8,12},{9,1},{1... | collective-permute-start | bytes 786440 | tf_op jit(solution)/shard_map/ppermute | solution.py:282
  54.0 4.9 %collective-permute-done.4.got_ref = bf16[256,512]{1,0:T(8,128)(2,1)S(1)} collective-permute-done((bf16[256,512]{1,0:T(8,128)(2,1)S(1)}, bf16[256,512]{1,0:T(8,128)(2,1)S(1)}, u32[]{:S(2)}, u32[]{:S(2)}) %collective-permute-start.4) | collective-permute-done | bytes 262176 | tf_op jit(solution)/shard_map/ppermute | solution.py:282
  58.9 0.3 collective-permute-start.5
  59.3 5.9 %collective-permute-done.5.got_ref = bf16[128,512]{1,0:T(8,128)(2,1)S(1)} collective-permute-done((bf16[128,512]{1,0:T(8,128)(2,1)S(1)}, bf16[128,512]{1,0:T(8,128)(2,1)S(1)}, u32[]{:S(2)}, u32[]{:S(2)}) %collective-permute-start.5) | collective-permute-done | bytes 131104 | tf_op jit(solution)/shard_map/ppermute | solution.py:282
  65.2 2.7 %collective-permute-start.6 = (bf16[64,512]{1,0:T(8,128)(2,1)S(1)}, bf16[64,512]{1,0:T(8,128)(2,1)S(1)}, u32[]{:S(2)}, u32[]{:S(2)}) collective-permute-start(bf16[64,512]{1,0:T(8,128)(2,1)S(1)} %get-tuple-element.55), channel_id=1, source_target_pairs={{0,16},{1,17},{2,18},{3,19},{4,20},{5,21},{6,22},{7,23},{8,24},{9,... | collective-permute-start | bytes 196616 | tf_op jit(solution)/shard_map/ppermute | solution.py:282
  67.8 1.8 %shard_map.97.near_ref = f32[512,1024]{1,0:T(8,128)S(1)} custom-call(bf16[512,1024]{1,0:T(8,128)(2,1)S(1)} %get-tuple-element.37.dq_ref.dqt_ref, bf16[512,1024]{1,0:T(8,128)(2,1)S(1)} %get-tuple-element.38.dkt_ref, bf16[512,1024]{1,0:T(8,128)(2,1)S(1)} %get-tuple-element.39.dvt_ref, bf16[512,512]{1,0:T(8,128)(2,1)S(1)} %get-tuple-element.40.wq_ref, ...), custom_call_target="tpu_custom_call" | custom-call | flops 1610612736 | bytes 4718592 | tf_op jit(solution)/shard_map/pallas_call | solution.py:249
  69.6 0.0 collective-permute-done.1.back_ref
  69.6 1.3 %shard_map.99 = bf16[1024,512]{1,0:T(8,128)(2,1)} custom-call(f32[512,1024]{1,0:T(8,128)S(1)} %shard_map.97.near_ref, bf16[512,1024]{1,0:T(8,128)(2,1)S(1)} %collective-permute-done.1.back_ref), custom_call_target="tpu_custom_call" | custom-call | flops 67108864 | bytes 3145728 | tf_op jit(solution)/shard_map/pallas_call | solution.py:249
  71.0 0.0 collective-permute-done.6.got_ref
  71.0 0.7 shard_map.105
  (2 shorter events, 0.1 us)
Async XLA Ops:
  0.6 20.8 %collective-permute-start = (bf16[1024,512]{1,0:T(8,128)(2,1)}, bf16[1024,512]{1,0:T(8,128)(2,1)S(1)}, u32[]{:S(2)}, u32[]{:S(2)}) collective-permute-start(bf16[1024,512]{1,0:T(8,128)(2,1)} %bitcast.8), channel_id=1, source_target_pairs={{0,1},{1,2},{2,3},{4,5},{5,6},{6,7},{8,9},{9,10},{10,11},{12,13},{... | collective-permute-start | bytes 3145736 | tf_op jit(solution)/shard_map/ppermute | solution.py:293
  38.1 4.9 %collective-permute-start.2 = (bf16[1024,512]{1,0:T(8,128)(2,1)S(1)}, bf16[1024,512]{1,0:T(8,128)(2,1)S(1)}, u32[]{:S(2)}, u32[]{:S(2)}) collective-permute-start(bf16[1024,512]{1,0:T(8,128)(2,1)S(1)} %get-tuple-element.47), channel_id=1, source_target_pairs={{0,1},{1,0},{2,3},{3,2},{4,5},{5,4},{6,7},{7,6},{8,9},{9,8},{10,11... | collective-permute-start | bytes 3145736 | tf_op jit(solution)/shard_map/ppermute | solution.py:270
  43.1 9.2 %collective-permute-start.3 = (bf16[512,512]{1,0:T(8,128)(2,1)S(1)}, bf16[512,512]{1,0:T(8,128)(2,1)S(1)}, u32[]{:S(2)}, u32[]{:S(2)}) collective-permute-start(bf16[512,512]{1,0:T(8,128)(2,1)S(1)} %get-tuple-element.49), channel_id=1, source_target_pairs={{0,8},{1,5},{2,10},{3,7},{4,12},{5,1},{6,14},{7,3},{8,0},{9,13},{1... | collective-permute-start | bytes 1572872 | tf_op jit(solution)/shard_map/ppermute | solution.py:282
  46.0 23.6 %collective-permute-start.1 = (bf16[512,1024]{1,0:T(8,128)(2,1)S(1)}, bf16[512,1024]{1,0:T(8,128)(2,1)S(1)}, u32[]{:S(2)}, u32[]{:S(2)}) collective-permute-start(bf16[512,1024]{1,0:T(8,128)(2,1)S(1)} %shard_map.98), channel_id=1, source_target_pairs={{1,0},{2,1},{3,2},{5,4},{6,5},{7,6},{9,8},{10,9},{11,10},{13,12},{... | collective-permute-start | bytes 3145736 | tf_op jit(solution)/shard_map/ppermute | solution.py:326
  52.4 6.4 %collective-permute-start.4 = (bf16[256,512]{1,0:T(8,128)(2,1)S(1)}, bf16[256,512]{1,0:T(8,128)(2,1)S(1)}, u32[]{:S(2)}, u32[]{:S(2)}) collective-permute-start(bf16[256,512]{1,0:T(8,128)(2,1)S(1)} %get-tuple-element.51), channel_id=1, source_target_pairs={{0,4},{1,9},{2,6},{3,11},{4,0},{5,13},{6,2},{7,15},{8,12},{9,1},{1... | collective-permute-start | bytes 786440 | tf_op jit(solution)/shard_map/ppermute | solution.py:282
  58.9 6.2 %collective-permute-start.5 = (bf16[128,512]{1,0:T(8,128)(2,1)S(1)}, bf16[128,512]{1,0:T(8,128)(2,1)S(1)}, u32[]{:S(2)}, u32[]{:S(2)}) collective-permute-start(bf16[128,512]{1,0:T(8,128)(2,1)S(1)} %get-tuple-element.53), channel_id=1, source_target_pairs={{0,2},{1,3},{2,0},{3,1},{4,6},{5,7},{6,4},{7,5},{8,10},{9,11},{10,... | collective-permute-start | bytes 393224 | tf_op jit(solution)/shard_map/ppermute | solution.py:282
  65.2 5.8 %collective-permute-start.6 = (bf16[64,512]{1,0:T(8,128)(2,1)S(1)}, bf16[64,512]{1,0:T(8,128)(2,1)S(1)}, u32[]{:S(2)}, u32[]{:S(2)}) collective-permute-start(bf16[64,512]{1,0:T(8,128)(2,1)S(1)} %get-tuple-element.55), channel_id=1, source_target_pairs={{0,16},{1,17},{2,18},{3,19},{4,20},{5,21},{6,22},{7,23},{8,24},{9,... | collective-permute-start | bytes 196616 | tf_op jit(solution)/shard_map/ppermute | solution.py:282
